TPU v7x, 32 devices: a whole 2x2x4 slice. The times are simulated.
32 devices in a mesh: groups: 2 (over y), dp: 4 (over z), ctx: 4 (over x, core).
Axes of the slice: x: 2, y: 2, z: 4, core: 2. Of those that a mesh axis runs over, the one named last changes fastest.
Arguments:
- queries: bfloat16 [8, 1024, 2048], P(('groups', 'dp'), 'ctx'), parts along dimension 0, may hold values from -480 to 480
- keys: bfloat16 [8, 1024, 256], P(('groups', 'dp'), 'ctx'), parts along dimension 0, may hold values from -4.1 to 4.1
- values: bfloat16 [8, 1024, 256], P(('groups', 'dp'), 'ctx'), parts along dimension 0, may hold values from -6 to 6
- grad_out: bfloat16 [8, 1024, 2048], P(('groups', 'dp'), 'ctx'), parts along dimension 0, may hold values from -6 to 6
- sinks: float32 [32], replicated, may hold values from 0 to 6
- doc_ids: int32 [8, 1024], P(('groups', 'dp')), parts along dimension 0, may hold values from 0 to 1, never falling along the last dimension, each value on 1 to 768 neighbouring positions
- swap_flags: int32 [8, 4, 16], P(('groups', 'dp'), 'ctx'), parts along dimension 0, may hold values from 0 to 1, as said below
Outputs:
- attn_out: bfloat16 [8, 1024, 2048], P(('groups', 'dp'), 'ctx'), parts along dimension 0
- grad_queries: bfloat16 [8, 1024, 2048], P(('groups', 'dp'), 'ctx'), parts along dimension 0
- grad_keys: bfloat16 [8, 1024, 256], P(('groups', 'dp'), 'ctx'), parts along dimension 0
- grad_values: bfloat16 [8, 1024, 256], P(('groups', 'dp'), 'ctx'), parts along dimension 0
There are 2 independent parts, one for each index of `groups`. A program takes and returns all parts, laid end to end along the dimension named above; an argument that names none is the same for every part. Nothing has to cross between parts.
Inputs may be any that keep to these rules, and one draw needn't show every extreme that they name: `doc_ids`: each of the 2 responses of a pack covers between 256 and 768 neighbouring positions. swap_flags of rank i and run c equal those of its partner rank (i + 2) mod 4 and run c; each device has at most 1 ones, and some device has exactly 1.
All inputs are finite; a program needn't handle non-finite values.
Results may differ from a plain program's by a relative error of at most 0.019.
Values may be sent and summed in bfloat16 or wider, within the bound.
No kernel may reach another device: no remote copies, remote signals or barrier semaphores. Data moves between devices by JAX's collectives and lax.ppermute only.
A program may use at most 64 MiB of HBM per device.

v0:
```python
import math

import jax
import jax.numpy as jnp
from jax import lax
from jax.sharding import PartitionSpec as P

QUERY_HEADS = 32
KEY_VALUE_HEADS = 4
HEAD_SIZE = 64
WINDOW = 128
CAP = 1


def swapped(block, axis, apart):
    count = lax.axis_size(axis)
    route = []
    for low in range(count):
        high = low | 1 << apart
        if high != low and high < count:
            route += [(low, high), (high, low)]
    return lax.ppermute(block, axis, route)


def shifted(value, axis, steps):
    count = lax.axis_size(axis)
    initial, last = (max(0, -steps), min(count, count - steps))
    return lax.ppermute(value, axis, [(source, source + steps) for source in range(initial, last)])


def reach_partner(outgoing):
    return swapped(outgoing, "dp", lax.axis_size("dp").bit_length() - 2)


def shards(queries, keys, values, grad_out, sinks, doc_ids, swap_flags):
    row_count = queries.shape[1]
    swap_marks = swap_flags[0, 0]
    block_count = swap_marks.shape[0]
    block_rows = row_count // block_count
    query_width = queries.shape[2]
    key_span_width = keys.shape[2]
    heads_per_group = QUERY_HEADS // KEY_VALUE_HEADS
    group_width = heads_per_group * HEAD_SIZE
    score_scale = 1.0 / math.sqrt(HEAD_SIZE)
    filled = jnp.cumsum(swap_marks) - 1
    slot_numbers = jnp.arange(CAP, dtype=jnp.int32)
    block_numbers = jnp.arange(block_count, dtype=jnp.int32)
    hits = (swap_marks[None, :] == 1) & (filled[None, :] == slot_numbers[:, None])
    chosen = jnp.sum(jnp.where(hits, block_numbers[None, :], 0), axis=1)
    landing = jnp.clip(filled, 0, CAP - 1)

    def trade(rows_data):
        width = rows_data.shape[1]
        blocked = rows_data.reshape(block_count, block_rows, width)
        outgoing = jnp.take(blocked, chosen, axis=0)
        incoming = reach_partner(outgoing)
        spread = jnp.take(incoming, landing, axis=0)
        return jnp.where(swap_marks[:, None, None] == 1, spread, blocked).reshape(row_count, width)

    bundle = trade(jnp.concatenate([queries[0], keys[0], values[0], grad_out[0]], axis=1))
    pack_q = bundle[:, :query_width]
    pack_k = bundle[:, query_width : query_width + key_span_width]
    pack_v = bundle[:, query_width + key_span_width : query_width + 2 * key_span_width]
    pack_g = bundle[:, query_width + 2 * key_span_width :]
    tail_rows = jnp.concatenate([pack_k, pack_v], axis=1)[row_count - WINDOW :]
    halo_rows = shifted(tail_rows, "ctx", 1)
    key_all = jnp.concatenate([halo_rows[:, :key_span_width], pack_k], axis=0)
    value_all = jnp.concatenate([halo_rows[:, key_span_width:], pack_v], axis=0)
    span = row_count + WINDOW
    offset = lax.axis_index("ctx") * row_count
    pack_docs = doc_ids[0]
    docs_pad = jnp.concatenate([jnp.full((WINDOW,), -1, jnp.int32), pack_docs], axis=0)
    query_docs = lax.dynamic_slice_in_dim(pack_docs, offset, row_count, 0)
    key_docs = lax.dynamic_slice_in_dim(docs_pad, offset, span, 0)
    distance = (
        jnp.arange(row_count, dtype=jnp.int32)[:, None]
        + WINDOW
        - jnp.arange(span, dtype=jnp.int32)[None, :]
    )
    allowed = (query_docs[:, None] == key_docs[None, :]) & (distance >= 0) & (distance < WINDOW)
    saved = []
    out_parts = []
    for key_value_group in range(KEY_VALUE_HEADS):
        query_group = pack_q[
            :, key_value_group * group_width : (key_value_group + 1) * group_width
        ].reshape(row_count, heads_per_group, HEAD_SIZE)
        key_group = key_all[:, key_value_group * HEAD_SIZE : (key_value_group + 1) * HEAD_SIZE]
        value_group = value_all[:, key_value_group * HEAD_SIZE : (key_value_group + 1) * HEAD_SIZE]
        sink_group = sinks[
            key_value_group * heads_per_group : (key_value_group + 1) * heads_per_group
        ][:, None]
        scores = (
            jnp.einsum("rgd,ld->grl", query_group, key_group, preferred_element_type=jnp.float32)
            * score_scale
        )
        masked = jnp.where(allowed, scores, jnp.float32(-1e30))
        top = jnp.maximum(jnp.max(masked, axis=-1), sink_group)
        expo = jnp.where(allowed, jnp.exp(masked - top[..., None]), jnp.float32(0.0))
        total = jnp.exp(sink_group - top) + jnp.sum(expo, axis=-1)
        probs = expo / total[..., None]
        probs_b = probs.astype(jnp.bfloat16)
        out_group = jnp.einsum(
            "grl,ld->rgd", probs_b, value_group, preferred_element_type=jnp.float32
        ).astype(jnp.bfloat16)
        saved.append((probs, probs_b, out_group))
        out_parts.append(out_group.reshape(row_count, group_width))
    pack_out = jnp.concatenate(out_parts, axis=1)
    final_out = trade(pack_out)
    dq_parts = []
    dk_parts = []
    dv_parts = []
    for key_value_group in range(KEY_VALUE_HEADS):
        probs, probs_b, out_group = saved[key_value_group]
        query_group = pack_q[
            :, key_value_group * group_width : (key_value_group + 1) * group_width
        ].reshape(row_count, heads_per_group, HEAD_SIZE)
        grad_group = pack_g[
            :, key_value_group * group_width : (key_value_group + 1) * group_width
        ].reshape(row_count, heads_per_group, HEAD_SIZE)
        key_group = key_all[:, key_value_group * HEAD_SIZE : (key_value_group + 1) * HEAD_SIZE]
        value_group = value_all[:, key_value_group * HEAD_SIZE : (key_value_group + 1) * HEAD_SIZE]
        row_dot = jnp.einsum(
            "rgd,rgd->gr", grad_group.astype(jnp.float32), out_group.astype(jnp.float32)
        )
        dprobs = jnp.einsum(
            "rgd,ld->grl", grad_group, value_group, preferred_element_type=jnp.float32
        )
        dscores_b = (probs * (dprobs - row_dot[..., None])).astype(jnp.bfloat16)
        query_gradient = (
            jnp.einsum("grl,ld->rgd", dscores_b, key_group, preferred_element_type=jnp.float32)
            * score_scale
        )
        dq_parts.append(query_gradient.astype(jnp.bfloat16).reshape(row_count, group_width))
        dk_parts.append(
            jnp.einsum("grl,rgd->ld", dscores_b, query_group, preferred_element_type=jnp.float32)
            * score_scale
        )
        dv_parts.append(
            jnp.einsum("grl,rgd->ld", probs_b, grad_group, preferred_element_type=jnp.float32)
        )
    pack_dq = jnp.concatenate(dq_parts, axis=1)
    grad_k_all = jnp.concatenate(dk_parts, axis=1)
    grad_v_all = jnp.concatenate(dv_parts, axis=1)
    returned = shifted(
        jnp.concatenate([grad_k_all[:WINDOW], grad_v_all[:WINDOW]], axis=1), "ctx", -1
    )
    grad_k_own = grad_k_all[WINDOW:].at[row_count - WINDOW :].add(returned[:, :key_span_width])
    grad_v_own = grad_v_all[WINDOW:].at[row_count - WINDOW :].add(returned[:, key_span_width:])
    pack_dk = grad_k_own.astype(jnp.bfloat16)
    pack_dv = grad_v_own.astype(jnp.bfloat16)
    gradients = trade(jnp.concatenate([pack_dq, pack_dk, pack_dv], axis=1))
    final_dq = gradients[:, :query_width]
    final_dk = gradients[:, query_width : query_width + key_span_width]
    final_dv = gradients[:, query_width + key_span_width :]
    return (final_out[None], final_dq[None], final_dk[None], final_dv[None])


def solution(mesh):
    in_specs = (
        P(("groups", "dp"), "ctx", None),
        P(("groups", "dp"), "ctx", None),
        P(("groups", "dp"), "ctx", None),
        P(("groups", "dp"), "ctx", None),
        P(),
        P(("groups", "dp"), None),
        P(("groups", "dp"), "ctx", None),
    )
    out_specs = (
        P(("groups", "dp"), "ctx", None),
        P(("groups", "dp"), "ctx", None),
        P(("groups", "dp"), "ctx", None),
        P(("groups", "dp"), "ctx", None),
    )
    return jax.shard_map(shards, mesh=mesh, in_specs=in_specs, out_specs=out_specs, check_vma=False)
```

profile of v0, /device:TPU:11, one launch (start us, length us, event | category | flops | bytes accessed | tf_op | source)
XLA Modules:
  0.0 97.5 jit_solution(12434777906133009077)
XLA Ops:
  0.7 0.9 copy.45
  1.7 1.3 %fusion.84 = s32[]{:T(128)} fusion(pred[16]{0:T(512)(128)(4,1)S(1)} %get-tuple-element.69, s32[1,1,16]{2,1,0:T(1,128)} %param.17), kind=kLoop, calls=%fused_computation.169 | loop fusion | flops 63 | bytes 84 | tf_op jit(solution)/shard_map/reduce_sum | solution.py:49
  5.0 1.6 %broadcast_select_fusion = bf16[1,16,4608]{2,1,0:T(8,128)(2,1)} fusion(pred[]{:T(512)} %bitcast.12, s32[]{:T(128)} %bitcast.17, bf16[16,16,2048]{2,1,0:T(8,128)(2,1)} %bitcast.285, bf16[16,16,256]{2,1,0:T(8,128)(2,1)} %bitcast.316, bf16[16,16,256]{2,1,0:T(8,128)(2,1)} %bitcast.315, bf16[16,16,2048]{2,1,0:T(8,128)(2,1)} %bitcast.284), kind=kLoop, calls=%fused_computation.109 | loop fusion | flops 663552 | bytes 2506757 | tf_op jit(solution)/shard_map/jit(_take)/select_n | solution.py:55
  6.6 2.3 %collective-permute-start = (bf16[1,16,4608]{2,1,0:T(8,128)(2,1)}, bf16[1,16,4608]{2,1,0:T(8,128)(2,1)S(1)}, u32[]{:S(2)}, u32[]{:S(2)}) collective-permute-start(bf16[1,16,4608]{2,1,0:T(8,128)(2,1)} %broadcast_select_fusion), channel_id=1, source_target_pairs={{0,8},{8,0},{4,12},{12,4},{1,9},{9,1},{5,13},{13,5},{2,10},{10,2},... | collective-permute-start | bytes 442376 | tf_op jit(solution)/shard_map/ppermute | solution.py:22
  9.5 1.7 %copy.48 = bf16[1,256,256]{1,2,0:T(8,128)(2,1)} copy(bf16[1,256,256]{2,1,0:T(8,128)(2,1)} %param.12) | data formatting | bytes 262144 | tf_op args[1]
  11.2 1.7 %copy.49 = bf16[1,256,256]{1,2,0:T(8,128)(2,1)} copy(bf16[1,256,256]{2,1,0:T(8,128)(2,1)} %param.13) | data formatting | bytes 262144 | tf_op args[2]
  13.4 1.3 %copy.50 = bf16[1,256,2048]{1,2,0:T(8,128)(2,1)} copy(bf16[1,256,2048]{2,1,0:T(8,128)(2,1)S(1)} %copy-done.1) | data formatting | bytes 2097152 | tf_op args[3]
  16.5 1.1 %broadcast.422 = bf16[16,16,4608]{2,1,0:T(8,128)(2,1)S(1)} broadcast(bf16[16,4608]{1,0:T(8,128)(2,1)} %bitcast.327), dimensions={1,2} | broadcast | bytes 2506752 | tf_op jit(solution)/shard_map/jit(_take)/gather | solution.py:57
  17.6 2.4 %copy.46 = bf16[256,4608]{0,1:T(8,128)(2,1)} copy(bf16[256,4608]{1,0:T(8,128)(2,1)S(1)} %bitcast.283) | data formatting | bytes 4718592 | tf_op jit(solution)/shard_map/jit(_take)/gather | solution.py:57
  20.0 2.4 %maximum_select_fusion = bf16[256,4608]{0,1:T(8,128)(2,1)S(1)} fusion(bf16[256,2048]{0,1:T(8,128)(2,1)} %bitcast.288, bf16[256,256]{0,1:T(8,128)(2,1)} %bitcast.318, bf16[256,256]{0,1:T(8,128)(2,1)} %bitcast.317, bf16[256,2048]{0,1:T(8,128)(2,1)S(1)} %bitcast.287, bf16[256,4608]{0,1:T(8,128)(2,1)} %copy.46, pred[256]{0:T(512)(128)(4,1)S(1)} %broadcast_in_dim.156, ...), kind=kLoop, calls=%fused_computation.24 | loop fusion | flops 11796480 | bytes 7078400 | tf_op jit(solution)/shard_map/jit(_where)/select_n | solution.py:58
  22.6 1.3 %collective-permute-start.1 = (bf16[128,512]{0,1:T(8,128)(2,1)S(1)}, bf16[128,512]{0,1:T(8,128)(2,1)S(1)}, u32[]{:S(2)}, u32[]{:S(2)}) collective-permute-start(bf16[128,512]{0,1:T(8,128)(2,1)S(1)} %slice.229), channel_id=1, source_target_pairs={{0,1},{1,2},{2,3},{4,5},{5,6},{6,7},{8,9},{9,10},{10,11},{12,13},{... | collective-permute-start | bytes 393224 | tf_op jit(solution)/shard_map/ppermute | solution.py:28
  23.9 1.9 %collective-permute-done.1 = bf16[128,512]{0,1:T(8,128)(2,1)S(1)} collective-permute-done((bf16[128,512]{0,1:T(8,128)(2,1)S(1)}, bf16[128,512]{0,1:T(8,128)(2,1)S(1)}, u32[]{:S(2)}, u32[]{:S(2)}) %collective-permute-start.1) | collective-permute-done | bytes 131104 | tf_op jit(solution)/shard_map/ppermute | solution.py:28
  27.8 2.3 %fusion.13 = (f32[8,256]{1,0:T(8,128)S(1)}, f32[8,256]{1,0:T(8,128)S(1)}, f32[8,256]{1,0:T(8,128)S(1)}, f32[8,256]{1,0:T(8,128)S(1)}, f32[384,256,8]{1,0,2:T(8,128)S(1)}) fusion(f32[384,256,8]{1,0,2:T(8,128)S(1)} %get-tuple-element.101, f32[8,256]{1,0:T(8,128)S(1)} %broadcast_maximum_fusion.3, pred[256,384]{0,1:T(8,128)(4,1)S(1)} %fusion.44, ...), kind=kOutput, calls=%fused_computation.30 | convolution fusion | flops 111763456 | bytes 13180928 | tf_op jit(solution)/shard_map/rgd,ld->grl/dot_general | solution.py:93
  30.4 2.4 %fusion.15 = (f32[8,256]{1,0:T(8,128)S(1)}, f32[8,256]{1,0:T(8,128)S(1)}, f32[8,256]{1,0:T(8,128)S(1)}) fusion(f32[384,256,8]{1,0,2:T(8,128)S(1)} %get-tuple-element.102, f32[8,256]{1,0:T(8,128)S(1)} %broadcast_maximum_fusion.2, pred[256,384]{0,1:T(8,128)(4,1)S(1)} %fusion.44, f32[8,256]{1,0:T(8,128)S(1)} %broadcast_maximum_fusion.1, ...), kind=kLoop, calls=%fused_computation.32 | loop fusion | flops 11790336 | bytes 9584640 | tf_op jit(solution)/shard_map/reduce_sum | solution.py:99
  33.0 1.1 %convolution_convert_fusion.1 = bf16[64,8,256]{2,0,1:T(8,128)(2,1)S(1)} fusion(bf16[256,256]{0,1:T(8,128)(2,1)S(1)} %get-tuple-element.89, bf16[128,256]{0,1:T(8,128)(2,1)S(1)} %get-tuple-element.95, f32[384,256,8]{1,0,2:T(8,128)S(1)} %fusion.81, f32[8,256]{1,0:T(8,128)S(1)} %exponential_add_fusion.1, f32[8,256]{1,0:T(8,128)S(1)} %broadcast_maximum_fusion.1, ...), kind=kOutput, calls=%fused_computation.48 | convolution fusion | flops 105611264 | bytes 3719168 | tf_op jit(solution)/shard_map/grl,ld->rgd/dot_general | solution.py:102
  34.1 1.1 %convolution_convert_fusion.2 = bf16[64,8,256]{2,0,1:T(8,128)(2,1)S(1)} fusion(bf16[256,256]{0,1:T(8,128)(2,1)S(1)} %get-tuple-element.89, bf16[128,256]{0,1:T(8,128)(2,1)S(1)} %get-tuple-element.95, f32[384,256,8]{1,0,2:T(8,128)S(1)} %get-tuple-element.102, f32[8,256]{1,0:T(8,128)S(1)} %exponential_add_fusion.2, f32[8,256]{1,0:T(8,128)S(1)} %broadcast_maximum_fusion.2, ...), kind=kOutput, calls=%fused_computation.49 | convolution fusion | flops 105611264 | bytes 3719168 | tf_op jit(solution)/shard_map/grl,ld->rgd/dot_general | solution.py:102
  35.2 1.1 %convolution_convert_fusion.3 = bf16[64,8,256]{2,0,1:T(8,128)(2,1)S(1)} fusion(bf16[256,256]{0,1:T(8,128)(2,1)S(1)} %get-tuple-element.89, bf16[128,256]{0,1:T(8,128)(2,1)S(1)} %get-tuple-element.95, f32[384,256,8]{1,0,2:T(8,128)S(1)} %get-tuple-element.101, f32[8,256]{1,0:T(8,128)S(1)} %exponential_add_fusion.3, f32[8,256]{1,0:T(8,128)S(1)} %broadcast_maximum_fusion.3, ...), kind=kOutput, calls=%fused_computation.50 | convolution fusion | flops 105611264 | bytes 3719168 | tf_op jit(solution)/shard_map/grl,ld->rgd/dot_general | solution.py:102
  36.3 1.1 %convolution_convert_fusion = bf16[64,8,256]{2,0,1:T(8,128)(2,1)S(1)} fusion(bf16[384,64,1]{0,1,2:T(8,128)(2,1)S(1)} %get-tuple-element.104, f32[384,256,8]{1,0,2:T(8,128)S(1)} %fusion.109, f32[8,256]{1,0:T(8,128)S(1)} %exponential_add_fusion, f32[8,256]{1,0:T(8,128)S(1)} %broadcast_maximum_fusion, pred[256,384]{0,1:T(8,128)(4,1)S(1)} %fusion.44), kind=kOutput, calls=%fused_computation.47 | convolution fusion | flops 105512960 | bytes 3571712 | tf_op jit(solution)/shard_map/grl,ld->rgd/dot_general | solution.py:102
  37.9 1.1 %convolution_bitcast_fusion = f32[384,64]{0,1:T(8,128)S(1)} fusion(bf16[256,8,64]{0,2,1:T(8,128)(2,1)S(1)} %bitcast.325, f32[384,256,8]{1,0,2:T(8,128)S(1)} %fusion.109, f32[8,256]{1,0:T(8,128)S(1)} %exponential_add_fusion, f32[8,256]{1,0:T(8,128)S(1)} %broadcast_maximum_fusion, pred[256,384]{0,1:T(8,128)(4,1)S(1)} %fusion.44), kind=kOutput, calls=%fused_computation.51 | convolution fusion | flops 105381888 | bytes 3620864 | tf_op jit(solution)/shard_map/grl,rgd->ld/dot_general | solution.py:139
  39.0 1.2 %fusion.1 = bf16[8,256,384]{1,2,0:T(8,128)(2,1)S(1)} fusion(bf16[384,64,1]{0,1,2:T(8,128)(2,1)S(1)} %get-tuple-element.104, bf16[256,8,64]{0,2,1:T(8,128)(2,1)S(1)} %bitcast.326, f32[8,256]{1,0:T(8,128)S(1)} %get-tuple-element.70, f32[8,256]{1,0:T(8,128)S(1)} %exponential_add_fusion, f32[8,256]{1,0:T(8,128)S(1)} %broadcast_maximum_fusion, ...), kind=kOutput, calls=%fused_computation.2 | convolution fusion | flops 106954752 | bytes 5152768 | tf_op jit(solution)/shard_map/rgd,ld->grl/dot_general | solution.py:125
  41.2 1.1 %convolution_bitcast_fusion.1 = f32[384,64]{0,1:T(8,128)S(1)} fusion(bf16[256,8,64]{0,2,1:T(8,128)(2,1)S(1)} %bitcast.323, f32[384,256,8]{1,0,2:T(8,128)S(1)} %fusion.81, f32[8,256]{1,0:T(8,128)S(1)} %exponential_add_fusion.1, f32[8,256]{1,0:T(8,128)S(1)} %broadcast_maximum_fusion.1, pred[256,384]{0,1:T(8,128)(4,1)S(1)} %fusion.44), kind=kOutput, calls=%fused_computation.52 | convolution fusion | flops 105381888 | bytes 3620864 | tf_op jit(solution)/shard_map/grl,rgd->ld/dot_general | solution.py:139
  42.3 1.2 %fusion.3 = bf16[8,256,384]{1,2,0:T(8,128)(2,1)S(1)} fusion(bf16[256,8,64]{0,2,1:T(8,128)(2,1)S(1)} %bitcast.324, f32[8,256]{1,0:T(8,128)S(1)} %get-tuple-element.78, bf16[256,256]{0,1:T(8,128)(2,1)S(1)} %get-tuple-element.89, bf16[128,256]{0,1:T(8,128)(2,1)S(1)} %get-tuple-element.95, f32[8,256]{1,0:T(8,128)S(1)} %exponential_add_fusion.1, ...), kind=kOutput, calls=%fused_computation.5 | convolution fusion | flops 107053056 | bytes 5300224 | tf_op jit(solution)/shard_map/rgd,ld->grl/dot_general | solution.py:125
  44.5 1.1 %convolution_bitcast_fusion.2 = f32[384,64]{0,1:T(8,128)S(1)} fusion(bf16[256,8,64]{0,2,1:T(8,128)(2,1)S(1)} %bitcast.321, f32[384,256,8]{1,0,2:T(8,128)S(1)} %get-tuple-element.102, f32[8,256]{1,0:T(8,128)S(1)} %exponential_add_fusion.2, f32[8,256]{1,0:T(8,128)S(1)} %broadcast_maximum_fusion.2, pred[256,384]{0,1:T(8,128)(4,1)S(1)} %fusion.44), kind=kOutput, calls=%fused_computation.53 | convolution fusion | flops 105381888 | bytes 3620864 | tf_op jit(solution)/shard_map/grl,rgd->ld/dot_general | solution.py:139
  45.6 1.2 %fusion.5 = bf16[8,256,384]{1,2,0:T(8,128)(2,1)S(1)} fusion(bf16[256,8,64]{0,2,1:T(8,128)(2,1)S(1)} %bitcast.322, f32[8,256]{1,0:T(8,128)S(1)} %get-tuple-element.80, bf16[256,256]{0,1:T(8,128)(2,1)S(1)} %get-tuple-element.89, bf16[128,256]{0,1:T(8,128)(2,1)S(1)} %get-tuple-element.95, f32[8,256]{1,0:T(8,128)S(1)} %exponential_add_fusion.2, ...), kind=kOutput, calls=%fused_computation.8 | convolution fusion | flops 107053056 | bytes 5300224 | tf_op jit(solution)/shard_map/rgd,ld->grl/dot_general | solution.py:125
  48.0 1.1 %convolution_bitcast_fusion.3 = f32[384,64]{0,1:T(8,128)S(1)} fusion(bf16[256,8,64]{0,2,1:T(8,128)(2,1)S(1)} %bitcast.319, f32[384,256,8]{1,0,2:T(8,128)S(1)} %get-tuple-element.101, f32[8,256]{1,0:T(8,128)S(1)} %exponential_add_fusion.3, f32[8,256]{1,0:T(8,128)S(1)} %broadcast_maximum_fusion.3, pred[256,384]{0,1:T(8,128)(4,1)S(1)} %fusion.44), kind=kOutput, calls=%fused_computation.54 | convolution fusion | flops 105381888 | bytes 3620864 | tf_op jit(solution)/shard_map/grl,rgd->ld/dot_general | solution.py:139
  49.1 1.2 %fusion.7 = bf16[8,256,384]{1,2,0:T(8,128)(2,1)S(1)} fusion(bf16[256,8,64]{0,2,1:T(8,128)(2,1)S(1)} %bitcast.320, f32[8,256]{1,0:T(8,128)S(1)} %get-tuple-element.82, bf16[256,256]{0,1:T(8,128)(2,1)S(1)} %get-tuple-element.89, bf16[128,256]{0,1:T(8,128)(2,1)S(1)} %get-tuple-element.95, f32[8,256]{1,0:T(8,128)S(1)} %exponential_add_fusion.3, ...), kind=kOutput, calls=%fused_computation.11 | convolution fusion | flops 107053056 | bytes 5300224 | tf_op jit(solution)/shard_map/rgd,ld->grl/dot_general | solution.py:125
  53.0 0.9 copy.82
  53.9 0.9 copy.83
  57.2 0.9 copy.60
  59.7 6.2 %collective-permute-start.3 = (f32[128,512]{0,1:T(8,128)}, f32[128,512]{0,1:T(8,128)}, u32[]{:S(2)}, u32[]{:S(2)}) collective-permute-start(f32[128,512]{0,1:T(8,128)} %pad_maximum_fusion.2), channel_id=1, source_target_pairs={{1,0},{2,1},{3,2},{5,4},{6,5},{7,6},{9,8},{10,9},{11,10},{13,12},{... | collective-permute-start | bytes 786440 | tf_op jit(solution)/shard_map/ppermute | solution.py:28
  66.2 1.0 %concatenate.125 = bf16[16,16,512]{2,1,0:T(8,128)(2,1)} reshape(bf16[256,8,64]{2,1,0:T(8,128)(2,1)S(1)} %copy.64) | data formatting | bytes 524288 | tf_op jit(solution)/shard_map/concatenate | solution.py:151
  67.5 1.0 %concatenate.126 = bf16[16,16,512]{2,1,0:T(8,128)(2,1)} reshape(bf16[256,8,64]{2,1,0:T(8,128)(2,1)S(1)} %copy.66) | data formatting | bytes 524288 | tf_op jit(solution)/shard_map/concatenate | solution.py:151
  68.9 1.0 %concatenate.127 = bf16[16,16,512]{2,1,0:T(8,128)(2,1)} reshape(bf16[256,8,64]{2,1,0:T(8,128)(2,1)S(1)} %copy.68) | data formatting | bytes 524288 | tf_op jit(solution)/shard_map/concatenate | solution.py:151
  70.2 1.0 %concatenate.128 = bf16[16,16,512]{2,1,0:T(8,128)(2,1)} reshape(bf16[256,8,64]{2,1,0:T(8,128)(2,1)S(1)} %copy.70) | data formatting | bytes 524288 | tf_op jit(solution)/shard_map/concatenate | solution.py:151
  73.9 3.0 %collective-permute-start.2 = (bf16[1,16,2048]{2,1,0:T(8,128)(2,1)S(1)}, bf16[1,16,2048]{2,1,0:T(8,128)(2,1)S(1)}, u32[]{:S(2)}, u32[]{:S(2)}) collective-permute-start(bf16[1,16,2048]{2,1,0:T(8,128)(2,1)S(1)} %broadcast_select_fusion.1), channel_id=1, source_target_pairs={{0,8},{8,0},{4,12},{12,4},{1,9},{9,1},{5,13},{13,5},{2,10},{10,2},... | collective-permute-start | bytes 196616 | tf_op jit(solution)/shard_map/ppermute | solution.py:22
  76.9 1.0 constant_dynamic-update-slice_fusion.5
  77.9 1.0 constant_dynamic-update-slice_fusion.11
  78.9 1.0 constant_dynamic-update-slice_fusion.4
  79.8 1.0 constant_dynamic-update-slice_fusion.3
  80.8 1.0 %constant_dynamic-update-slice_fusion.2 = bf16[16,16,2560]{2,1,0:T(8,128)(2,1)S(1)} fusion(bf16[16,16,2560]{2,1,0:T(8,128)(2,1)S(1)} %constant_dynamic-update-slice_fusion.3, bf16[16,16,512]{2,1,0:T(8,128)(2,1)} %concatenate.128), kind=kLoop, calls=%fused_computation.139 | loop fusion | bytes 524288
  81.8 1.2 %constant_dynamic-update-slice_fusion.10 = bf16[256,2560]{1,0:T(8,128)(2,1)S(1)} fusion(bf16[256,2560]{1,0:T(8,128)(2,1)S(1)} %constant_dynamic-update-slice_fusion.11, bf16[256,512]{1,0:T(8,128)(2,1)} %copy.82), kind=kLoop, calls=%fused_computation.147 | loop fusion | bytes 524288
  83.0 1.0 constant_dynamic-update-slice_fusion.9
  84.0 1.0 constant_dynamic-update-slice_fusion.8
  85.1 1.4 %maximum_select_fusion.1 = bf16[1,256,2048]{2,1,0:T(8,128)(2,1)} fusion(bf16[1,256,512]{2,1,0:T(8,128)(2,1)S(1)} %copy-done.3, bf16[1,256,512]{2,1,0:T(8,128)(2,1)S(1)} %copy-done.5, bf16[1,256,512]{2,1,0:T(8,128)(2,1)S(1)} %copy-done.4, bf16[1,256,512]{2,1,0:T(8,128)(2,1)S(1)} %copy-done.2, pred[256]{0:T(512)(128)(4,1)S(1)} %broadcast_in_dim.156, ...), kind=kLoop, calls=%fused_computation.64 | loop fusion | flops 5242880 | bytes 3146240 | tf_op jit(solution)/shard_map/jit(_where)/select_n | solution.py:58
  86.5 1.0 %fusion.48 = (bf16[256,256]{0,1:T(8,128)(2,1)S(1)}, bf16[256,256]{0,1:T(8,128)(2,1)S(1)}) fusion(bf16[256,256]{0,1:T(8,128)(2,1)S(1)} %slice.259, f32[128,512]{0,1:T(8,128)} %collective-permute-done.3, f32[384,256]{0,1:T(8,128)S(1)} %pad_maximum_fusion.1, bf16[256,256]{0,1:T(8,128)(2,1)S(1)} %copy-done.6, f32[384,256]{0,1:T(8,128)S(1)} %pad_maximum_fusion), kind=kLoop, calls=%fused_computation.113 | loop fusion | flops 65536 | bytes 786432 | tf_op jit(solution)/shard_map/scatter-add | solution.py:148
  89.1 0.9 dynamic-slice_select_fusion
  90.2 5.2 %collective-permute-done.4 = bf16[1,16,2560]{2,1,0:T(8,128)(2,1)S(1)} collective-permute-done((bf16[1,16,2560]{2,1,0:T(8,128)(2,1)S(1)}, bf16[1,16,2560]{2,1,0:T(8,128)(2,1)S(1)}, u32[]{:S(2)}, u32[]{:S(2)}) %collective-permute-start.4) | collective-permute-done | bytes 81952 | tf_op jit(solution)/shard_map/ppermute | solution.py:22
  96.4 1.1 %slice_bitcast_fusion = bf16[1,256,2048]{2,1,0:T(8,128)(2,1)} fusion(bf16[256,2560]{1,0:T(8,128)(2,1)S(1)} %fusion.20), kind=kLoop, calls=%fused_computation.63 | loop fusion | bytes 2097152 | tf_op jit(solution)/shard_map/broadcast_in_dim | solution.py:155
  (98 shorter events, 22.6 us)
Async XLA Ops:
  0.6 12.2 %copy-start = (bf16[1,256,2048]{2,1,0:T(8,128)(2,1)S(1)}, bf16[1,256,2048]{2,1,0:T(8,128)(2,1)}, u32[]{:S(2)}) copy-start(bf16[1,256,2048]{2,1,0:T(8,128)(2,1)} %param.11) | copy-start | bytes 3145732
  0.6 12.8 %copy-start.1 = (bf16[1,256,2048]{2,1,0:T(8,128)(2,1)S(1)}, bf16[1,256,2048]{2,1,0:T(8,128)(2,1)}, u32[]{:S(2)}) copy-start(bf16[1,256,2048]{2,1,0:T(8,128)(2,1)} %param.14) | copy-start | bytes 3145732
  4.9 10.1 %copy-start.10 = (s32[1,1024]{1,0:T(1,128)S(1)}, s32[1,1024]{1,0:T(1,128)}, u32[]{:S(2)}) copy-start(s32[1,1024]{1,0:T(1,128)} %param.16) | copy-start | bytes 12292
  5.0 10.3 %copy-start.9 = (f32[32]{0:T(128)S(1)}, f32[32]{0:T(128)}, u32[]{:S(2)}) copy-start(f32[32]{0:T(128)} %param.15) | copy-start | bytes 388
  6.6 9.2 %collective-permute-start = (bf16[1,16,4608]{2,1,0:T(8,128)(2,1)}, bf16[1,16,4608]{2,1,0:T(8,128)(2,1)S(1)}, u32[]{:S(2)}, u32[]{:S(2)}) collective-permute-start(bf16[1,16,4608]{2,1,0:T(8,128)(2,1)} %broadcast_select_fusion), channel_id=1, source_target_pairs={{0,8},{8,0},{4,12},{12,4},{1,9},{9,1},{5,13},{13,5},{2,10},{10,2},... | collective-permute-start | bytes 442376 | tf_op jit(solution)/shard_map/ppermute | solution.py:22
  15.8 0.7 copy-start.7
  22.6 3.3 %collective-permute-start.1 = (bf16[128,512]{0,1:T(8,128)(2,1)S(1)}, bf16[128,512]{0,1:T(8,128)(2,1)S(1)}, u32[]{:S(2)}, u32[]{:S(2)}) collective-permute-start(bf16[128,512]{0,1:T(8,128)(2,1)S(1)} %slice.229), channel_id=1, source_target_pairs={{0,1},{1,2},{2,3},{4,5},{5,6},{6,7},{8,9},{9,10},{10,11},{12,13},{... | collective-permute-start | bytes 393224 | tf_op jit(solution)/shard_map/ppermute | solution.py:28
  59.7 26.8 %collective-permute-start.3 = (f32[128,512]{0,1:T(8,128)}, f32[128,512]{0,1:T(8,128)}, u32[]{:S(2)}, u32[]{:S(2)}) collective-permute-start(f32[128,512]{0,1:T(8,128)} %pad_maximum_fusion.2), channel_id=1, source_target_pairs={{1,0},{2,1},{3,2},{5,4},{6,5},{7,6},{9,8},{10,9},{11,10},{13,12},{... | collective-permute-start | bytes 786440 | tf_op jit(solution)/shard_map/ppermute | solution.py:28
  73.8 11.3 %copy-start.2 = (bf16[1,256,512]{2,1,0:T(8,128)(2,1)S(1)}, bf16[1,256,512]{2,1,0:T(8,128)(2,1)}, u32[]{:S(2)}) copy-start(bf16[1,256,512]{2,1,0:T(8,128)(2,1)} %copy.59) | copy-start | bytes 786436
  73.8 11.3 %copy-start.3 = (bf16[1,256,512]{2,1,0:T(8,128)(2,1)S(1)}, bf16[1,256,512]{2,1,0:T(8,128)(2,1)}, u32[]{:S(2)}) copy-start(bf16[1,256,512]{2,1,0:T(8,128)(2,1)} %copy.62) | copy-start | bytes 786436
  73.8 11.3 %copy-start.4 = (bf16[1,256,512]{2,1,0:T(8,128)(2,1)S(1)}, bf16[1,256,512]{2,1,0:T(8,128)(2,1)}, u32[]{:S(2)}) copy-start(bf16[1,256,512]{2,1,0:T(8,128)(2,1)} %copy.60) | copy-start | bytes 786436
  73.9 11.3 %copy-start.5 = (bf16[1,256,512]{2,1,0:T(8,128)(2,1)S(1)}, bf16[1,256,512]{2,1,0:T(8,128)(2,1)}, u32[]{:S(2)}) copy-start(bf16[1,256,512]{2,1,0:T(8,128)(2,1)} %copy.61) | copy-start | bytes 786436
  73.9 11.1 %collective-permute-start.2 = (bf16[1,16,2048]{2,1,0:T(8,128)(2,1)S(1)}, bf16[1,16,2048]{2,1,0:T(8,128)(2,1)S(1)}, u32[]{:S(2)}, u32[]{:S(2)}) collective-permute-start(bf16[1,16,2048]{2,1,0:T(8,128)(2,1)S(1)} %broadcast_select_fusion.1), channel_id=1, source_target_pairs={{0,8},{8,0},{4,12},{12,4},{1,9},{9,1},{5,13},{13,5},{2,10},{10,2},... | collective-permute-start | bytes 196616 | tf_op jit(solution)/shard_map/ppermute | solution.py:22
  80.8 5.7 %copy-start.6 = (bf16[256,256]{0,1:T(8,128)(2,1)S(1)}, bf16[256,256]{0,1:T(8,128)(2,1)}, u32[]{:S(2)}) copy-start(bf16[256,256]{0,1:T(8,128)(2,1)} %slice.254) | copy-start | bytes 393220
  81.8 3.1 %copy-start.8 = (bf16[16,16,2560]{2,1,0:T(8,128)(2,1)}, bf16[16,16,2560]{2,1,0:T(8,128)(2,1)S(1)}, u32[]{:S(2)}) copy-start(bf16[16,16,2560]{2,1,0:T(8,128)(2,1)S(1)} %constant_dynamic-update-slice_fusion.2) | copy-start | bytes 3932164
  90.0 5.4 %collective-permute-start.4 = (bf16[1,16,2560]{2,1,0:T(8,128)(2,1)S(1)}, bf16[1,16,2560]{2,1,0:T(8,128)(2,1)S(1)}, u32[]{:S(2)}, u32[]{:S(2)}) collective-permute-start(bf16[1,16,2560]{2,1,0:T(8,128)(2,1)S(1)} %dynamic-slice_select_fusion), channel_id=1, source_target_pairs={{0,8},{8,0},{4,12},{12,4},{1,9},{9,1},{5,13},{13,5},{2,10},{10,2},... | collective-permute-start | bytes 245768 | tf_op jit(solution)/shard_map/ppermute | solution.py:22
where the time goes:
time: 98.1 us; the launch traced here: 97.5 us
  local copies, waits for them, and re-layouts  37.8 us (39%)
  matrix products  21.9 us (22%)
  other arithmetic  14.1 us (14%)
  starting transfers between devices  13 us (13%)
  waiting for transfers between devices  7.58 us (8%)
  between operations  3.16 us (3%)
    unnamed x36, local copies, waits for them, and re-layouts  14.5 us
    concatenate x10, local copies, waits for them, and re-layouts, shards(): gradients = trade(jnp.concatenate([pack_dq, pack_dk, pack_dv], axis=1))  8.2 us
    ppermute x2, starting transfers between devices, shifted(): lax.ppermute(value, axis, [(source, source + steps) for source in range(i...  7.46 us
    ppermute x3, waiting for transfers between devices, swapped(): return lax.ppermute(block, axis, route)  5.64 us
    ppermute x3, starting transfers between devices, swapped(): return lax.ppermute(block, axis, route)  5.5 us
    dot_general x4, matrix products, shards(): jnp.einsum('rgd,ld->grl', grad_group, value_group, preferred_element_type...  4.91 us
    concatenate x8, local copies, waits for them, and re-layouts, shards(): pack_out = jnp.concatenate(out_parts, axis=1)  4.66 us
    dot_general x4, matrix products, shards(): jnp.einsum('grl,ld->rgd', probs_b, value_group, preferred_element_type=jn...  4.39 us
  transfers between devices with their start and end apart: 5, of which 3 were waited for; matrix products, arithmetic and copies ran while one was open for 24% of the time, Pallas kernels for 0%

commit v1 on v0

v1 whole, which is shorter than its diff:
```python
import functools
import math

import jax
import jax.numpy as jnp
from jax import lax
from jax.experimental import pallas as pl
from jax.experimental.pallas import tpu as pltpu
from jax.sharding import PartitionSpec as P

QUERY_HEADS = 32
KEY_VALUE_HEADS = 4
HEAD_SIZE = 64
WINDOW = 128
TILE = 128
SPAN = TILE + WINDOW
PAIR = 2 * HEAD_SIZE
GROUP = QUERY_HEADS // KEY_VALUE_HEADS
PAIRS = GROUP // 2
HALVES = KEY_VALUE_HEADS // 2
NEG = -1e30
F32 = jnp.float32
BF16 = jnp.bfloat16


def mm(a, b):
    return lax.dot_general(a, b, (((1,), (0,)), ((), ())), preferred_element_type=F32)


def mm_nt(a, b):
    return lax.dot_general(a, b, (((1,), (1,)), ((), ())), preferred_element_type=F32)


def low_lanes(rows, lanes=PAIR):
    return lax.broadcasted_iota(jnp.int32, (rows, lanes), 1) < HEAD_SIZE


def spread_head(pair, odd):
    wide = pair.astype(F32)
    low = low_lanes(wide.shape[0])
    if odd:
        high = jnp.where(low, 0.0, wide)
        return pltpu.roll(high, HEAD_SIZE, 1), high
    lower = jnp.where(low, wide, 0.0)
    return lower, pltpu.roll(lower, HEAD_SIZE, 1)


def head_operands(k_pair, v_pair, odd):
    rows = k_pair.shape[0]
    scale = 1.0 / math.sqrt(HEAD_SIZE)
    k_lo, k_hi = spread_head(k_pair, odd)
    v_lo, v_hi = spread_head(v_pair, odd)
    low = low_lanes(rows)
    ones_lo = jnp.where(low, 1.0, 0.0)
    ones_hi = jnp.where(low, 0.0, 1.0)
    return (
        (k_lo * scale).astype(BF16),
        (k_hi * scale).astype(BF16),
        jnp.concatenate([v_lo, ones_lo], axis=1).astype(BF16),
        jnp.concatenate([v_hi, ones_hi], axis=1).astype(BF16),
    )


def attend_pair(q, g, operands, bias, sink_even, sink_odd):
    k_lo, k_hi, v_lo, v_hi = operands
    rows = q.shape[0]
    low = low_lanes(rows)
    expos, tops = [], []
    for k_half, sink in ((k_lo, sink_even), (k_hi, sink_odd)):
        scores = mm_nt(q, k_half) + bias
        top = jnp.maximum(jnp.max(scores, axis=1, keepdims=True), sink)
        expos.append(jnp.exp(scores - top))
        tops.append(jnp.exp(sink - top))
    rounded = [expo.astype(BF16) for expo in expos]
    mixed = mm(rounded[0], v_lo) + mm(rounded[1], v_hi)
    inverse = 1.0 / (mixed[:, PAIR:] + jnp.where(low, tops[0], tops[1]))
    out = (mixed[:, :PAIR] * inverse).astype(BF16)
    weighted = (g.astype(F32) * inverse).astype(BF16)
    product = weighted.astype(F32) * out.astype(F32)
    dots = (
        jnp.sum(jnp.where(low, product, 0.0), axis=1, keepdims=True),
        jnp.sum(jnp.where(low, 0.0, product), axis=1, keepdims=True),
    )
    deltas = []
    for expo, dot, v_half in ((expos[0], dots[0], v_lo), (expos[1], dots[1], v_hi)):
        deltas.append((expo * (mm_nt(weighted, v_half[:, :PAIR]) - dot)).astype(BF16))
    dq = (mm(deltas[0], k_lo) + mm(deltas[1], k_hi)).astype(BF16)
    return out, dq, weighted, rounded, deltas


def key_sums(stacked, both):
    turned = jnp.transpose(stacked)
    return mm(
        jnp.concatenate([turned[:HEAD_SIZE], turned[HEAD_SIZE:]], axis=1),
        jnp.concatenate(both, axis=0),
    )


def tile_work(q_ref, g_ref, sinks_ref, k_ext, v_ext, bias, out_ref, dq_ref, half):
    dk_parts, dv_parts = [], []
    for odd in range(2):
        operands = head_operands(k_ext, v_ext, odd)
        dk = dv = None
        for pair in range(PAIRS):
            head = odd * GROUP + 2 * pair
            lanes = slice(head * HEAD_SIZE, (head + 2) * HEAD_SIZE)
            index = half * (2 * GROUP) + head
            q = q_ref[:, lanes]
            out, dq, weighted, rounded, deltas = attend_pair(
                q, g_ref[:, lanes], operands, bias, sinks_ref[index], sinks_ref[index + 1]
            )
            out_ref[:, lanes] = out
            dq_ref[:, lanes] = dq
            dk_one = key_sums(q, deltas)
            dv_one = key_sums(weighted, rounded)
            dk = dk_one if dk is None else dk + dk_one
            dv = dv_one if dv is None else dv + dv_one
        dk_parts.append(dk)
        dv_parts.append(dv)
    scale = 1.0 / math.sqrt(HEAD_SIZE)
    return (
        jnp.transpose(jnp.concatenate(dk_parts, axis=0)) * scale,
        jnp.transpose(jnp.concatenate(dv_parts, axis=0)),
    )


def flagged(flags_ref, count):
    amount = flags_ref[0]
    number = jnp.int32(0)
    for block in range(1, count):
        amount = amount + flags_ref[block]
        number = number + flags_ref[block] * block
    return amount, number


def pick_kernel(blocks, first_tail, flags_ref, q_ref, g_ref, k_ref, v_ref, kt_ref, vt_ref, qg_ref, kv_ref, tail_ref):
    amount, number = flagged(flags_ref, blocks)
    wide = q_ref.shape[1]
    qg_ref[:, :wide] = q_ref[...]
    qg_ref[:, wide:] = g_ref[...]
    kv_ref[:, :PAIR] = k_ref[...]
    kv_ref[:, PAIR:] = v_ref[...]
    tail_ref[:WINDOW, :PAIR] = kt_ref[...]
    tail_ref[:WINDOW, PAIR:] = vt_ref[...]
    mark = jnp.where(amount * number >= first_tail, number - first_tail + 1, 0)
    tail_ref[WINDOW:, :] = jnp.full((tail_ref.shape[0] - WINDOW, 2 * PAIR), mark.astype(F32)).astype(BF16)


def fill_own(own_ref, blocks, block_rows, flags_ref, incoming_ref, kv_scr, base):
    amount, number = flagged(flags_ref, blocks)
    own_k, own_v = own_ref
    rows = own_k.shape[0]
    kv_scr[base : base + rows, :PAIR] = own_k[...]
    kv_scr[base : base + rows, PAIR:] = own_v[...]

    @pl.when(amount > 0)
    def _():
        start = pl.multiple_of(base + number * block_rows, block_rows)
        kv_scr[pl.ds(start, block_rows), :] = incoming_ref[...]

    return amount, number


def fill_halo(tail_ref, cross_ref, block_rows, kv_scr):
    kv_scr[:WINDOW, :] = tail_ref[:WINDOW, :]
    mark = jnp.max(tail_ref[WINDOW:, :].astype(F32)).astype(jnp.int32)

    @pl.when(mark > 0)
    def _():
        start = pl.multiple_of((mark - 1) * block_rows, block_rows)
        kv_scr[pl.ds(start, block_rows), :] = cross_ref[...]

    return mark


def late_kernel(blocks, block_rows, flags_ref, sinks_ref, q_ref, g_ref, k_ref, v_ref, kv_ref, bias_ref, out_ref, dq_ref, dkv_ref, kv_scr):
    fill_own((k_ref, v_ref), blocks, block_rows, flags_ref, kv_ref, kv_scr, 0)
    kv = kv_scr[...]
    dk, dv = tile_work(q_ref, g_ref, sinks_ref, kv[:, :PAIR], kv[:, PAIR:], bias_ref[...], out_ref, dq_ref, pl.program_id(0))
    dkv_ref[:, :PAIR] = dk
    dkv_ref[:, PAIR:] = dv


def swap_kernel(blocks, block_rows, flags_ref, sinks_ref, qg_ref, k_ref, v_ref, kv_ref, tail_ref, cross_ref, bias_ref, oq_ref, dkv_ref, kv_scr):
    half = pl.program_id(0)
    _, number = fill_own((k_ref, v_ref), blocks, block_rows, flags_ref, kv_ref, kv_scr, WINDOW)
    fill_halo(tail_ref, cross_ref, block_rows, kv_scr)
    limit = kv_scr.shape[0] - SPAN
    start = pl.multiple_of(jnp.minimum(number * block_rows, limit), block_rows)
    kv = kv_scr[pl.ds(start, SPAN), :]
    wide = qg_ref.shape[1] // 2
    bias = bias_ref[...]
    scale = 1.0 / math.sqrt(HEAD_SIZE)
    dk_parts, dv_parts = [], []
    for odd in range(2):
        operands = head_operands(kv[:, :PAIR], kv[:, PAIR:], odd)
        first = odd * GROUP
        spots = [slice((first + 2 * pair) * HEAD_SIZE, (first + 2 * pair + 2) * HEAD_SIZE) for pair in range(PAIRS)]
        q = jnp.concatenate([qg_ref[:, spot] for spot in spots], axis=0)
        g = jnp.concatenate([qg_ref[:, wide + spot.start : wide + spot.stop] for spot in spots], axis=0)
        base = half * (2 * GROUP) + first
        sinks = [
            jnp.concatenate(
                [jnp.full((block_rows, 1), sinks_ref[base + 2 * pair + side], F32) for pair in range(PAIRS)], axis=0
            )
            for side in range(2)
        ]
        out, dq, weighted, rounded, deltas = attend_pair(q, g, operands, bias, sinks[0], sinks[1])
        for pair, spot in enumerate(spots):
            rows = slice(pair * block_rows, (pair + 1) * block_rows)
            oq_ref[:, spot] = out[rows]
            oq_ref[:, wide + spot.start : wide + spot.stop] = dq[rows]
        q_t = jnp.transpose(q.astype(F32)).astype(BF16)
        w_t = jnp.transpose(weighted.astype(F32)).astype(BF16)
        dk_parts.append(mm(q_t[:HEAD_SIZE], deltas[0]) + mm(q_t[HEAD_SIZE:], deltas[1]))
        dv_parts.append(mm(w_t[:HEAD_SIZE], rounded[0]) + mm(w_t[HEAD_SIZE:], rounded[1]))
    dkv_ref[:, :PAIR] = jnp.transpose(jnp.concatenate(dk_parts, axis=0)) * scale
    dkv_ref[:, PAIR:] = jnp.transpose(jnp.concatenate(dv_parts, axis=0))


def early_kernel(
    blocks, block_rows, flags_ref, sinks_ref, q_ref, g_ref, k_ref, v_ref, kv_ref, tail_ref, cross_ref, bias_ref,
    late_ref, swap_ref, out_in, dq_in, out_ref, dq_ref, own_ref, back_ref, cross_back_ref, trade_ref, kv_scr, dkv_scr,
):
    amount, number = fill_own((k_ref, v_ref), blocks, block_rows, flags_ref, kv_ref, kv_scr, WINDOW)
    mark = fill_halo(tail_ref, cross_ref, block_rows, kv_scr)
    kv = kv_scr[:SPAN, :]
    dk, dv = tile_work(q_ref, g_ref, sinks_ref, kv[:, :PAIR], kv[:, PAIR:], bias_ref[...], out_ref, dq_ref, pl.program_id(0))
    own_rows = late_ref.shape[0]
    dkv_scr[:WINDOW, :PAIR] = dk[:WINDOW]
    dkv_scr[:WINDOW, PAIR:] = dv[:WINDOW]
    dkv_scr[WINDOW:SPAN, :PAIR] = dk[WINDOW:] + late_ref[:TILE, :PAIR]
    dkv_scr[WINDOW:SPAN, PAIR:] = dv[WINDOW:] + late_ref[:TILE, PAIR:]
    dkv_scr[SPAN:, :] = late_ref[TILE:, :]

    @pl.when(amount > 0)
    def _():
        limit = dkv_scr.shape[0] - SPAN
        start = pl.multiple_of(jnp.minimum(number * block_rows, limit), block_rows)
        dkv_scr[pl.ds(start, SPAN), :] = dkv_scr[pl.ds(start, SPAN), :] + swap_ref[...]

    own_ref[...] = dkv_scr[WINDOW:, :]
    back_ref[...] = dkv_scr[:WINDOW, :].astype(BF16)
    spot = pl.multiple_of(WINDOW + number * block_rows, block_rows)
    trade_ref[...] = dkv_scr[pl.ds(spot, block_rows), :].astype(BF16)
    cross = pl.multiple_of(jnp.maximum(mark - 1, 0) * block_rows, block_rows)
    cross_back_ref[...] = dkv_scr[pl.ds(cross, block_rows), :].astype(BF16)


def finish_kernel(
    blocks, block_rows, flags_ref, oq_ref, own_ref, back_ref, cross_ref, trade_ref, out_in, dq_in,
    out_ref, dq_ref, dk_ref, dv_ref, sem,
):
    amount, number = flagged(flags_ref, blocks)
    start = pl.multiple_of(number * block_rows, block_rows)
    width = oq_ref.shape[1] // (2 * HALVES)
    copies = []
    for half in range(HALVES):
        for side, target in enumerate((out_ref, dq_ref)):
            lanes = (2 * half + side) * width
            copies.append(
                pltpu.make_async_copy(
                    oq_ref.at[:, pl.ds(lanes, width)],
                    target.at[pl.ds(start, block_rows), pl.ds(half * width, width)],
                    sem.at[2 * half + side],
                )
            )

    @pl.when(amount > 0)
    def _():
        for copy in copies:
            copy.start()

    rows = own_ref.shape[0]
    tail = rows - WINDOW
    for half in range(HALVES):
        for side, target in enumerate((dk_ref, dv_ref)):
            source = slice((2 * half + side) * PAIR, (2 * half + side + 1) * PAIR)
            lanes = slice(half * PAIR, (half + 1) * PAIR)
            target[:tail, lanes] = own_ref[:tail, source].astype(BF16)
            target[tail:, lanes] = (own_ref[tail:, source] + back_ref[:, source].astype(F32)).astype(BF16)

    @pl.when(amount > 0)
    def _():
        tail_part = jnp.where(start >= tail, 1.0, 0.0)
        for half in range(HALVES):
            for side, target in enumerate((dk_ref, dv_ref)):
                source = slice((2 * half + side) * PAIR, (2 * half + side + 1) * PAIR)
                lanes = slice(half * PAIR, (half + 1) * PAIR)
                total = trade_ref[:, source].astype(F32) + tail_part * cross_ref[:, source].astype(F32)
                target[pl.ds(start, block_rows), lanes] = total.astype(BF16)
        for copy in copies:
            copy.wait()


def shards(queries, keys, values, grad_out, sinks, doc_ids, swap_flags):
    rows, query_width = queries.shape[1:]
    key_width = keys.shape[2]
    flags = swap_flags[0, 0]
    blocks = flags.shape[0]
    block_rows = rows // blocks
    first_tail = (rows - WINDOW) // block_rows
    late_tile = rows // TILE - 1
    q, k, v, g = queries[0], keys[0], values[0], grad_out[0]
    wide = query_width // HALVES
    packs = lax.axis_size("dp")
    runs = lax.axis_size("ctx")
    partner = [(rank, (rank + packs // 2) % packs) for rank in range(packs)]
    forward = [(run, run + 1) for run in range(runs - 1)]
    across = [
        (rank * runs + run, (rank + packs // 2) % packs * runs + run + 1)
        for rank in range(packs)
        for run in range(runs - 1)
    ]

    def number_of(flags_ref):
        return sum(flags_ref[block] * block for block in range(1, blocks))

    def spec(shape, index):
        return pl.BlockSpec(shape, index)

    half_specs = lambda height, width, row=0: spec((height, width), lambda s, *_: (row, s))
    params = dict(compiler_params=pltpu.CompilerParams(dimension_semantics=("arbitrary",)))
    any_spec = pl.BlockSpec(memory_space=pl.ANY)

    qg_out, kv_out, tail_out = pl.pallas_call(
        functools.partial(pick_kernel, blocks, first_tail),
        grid_spec=pltpu.PrefetchScalarGridSpec(
            num_scalar_prefetch=1,
            grid=(HALVES,),
            in_specs=[
                spec((block_rows, wide), lambda s, f: (number_of(f), s)),
                spec((block_rows, wide), lambda s, f: (number_of(f), s)),
                spec((block_rows, PAIR), lambda s, f: (number_of(f), s)),
                spec((block_rows, PAIR), lambda s, f: (number_of(f), s)),
                half_specs(WINDOW, PAIR, rows // WINDOW - 1),
                half_specs(WINDOW, PAIR, rows // WINDOW - 1),
            ],
            out_specs=[
                half_specs(block_rows, 2 * wide),
                half_specs(block_rows, 2 * PAIR),
                half_specs(WINDOW + block_rows, 2 * PAIR),
            ],
        ),
        out_shape=[
            jax.ShapeDtypeStruct((block_rows, 2 * query_width), BF16),
            jax.ShapeDtypeStruct((block_rows, 2 * key_width), BF16),
            jax.ShapeDtypeStruct((WINDOW + block_rows, 2 * key_width), BF16),
        ],
        cost_estimate=pl.CostEstimate(flops=0, bytes_accessed=1 << 20, transcendentals=0),
        name="pick",
        **params,
    )(flags, q, g, k, v, k, v)

    kv_in = lax.ppermute(kv_out, "dp", partner)
    tail_in = lax.ppermute(tail_out, "ctx", forward)
    cross_in = lax.ppermute(kv_out, ("dp", "ctx"), across)
    qg_in = lax.ppermute(qg_out, "dp", partner)

    run = lax.axis_index("ctx")
    pack_docs = doc_ids[0]
    docs_pad = jnp.concatenate([jnp.full((WINDOW,), -1, jnp.int32), pack_docs])
    docs = lax.dynamic_slice_in_dim(docs_pad, run * rows, rows + WINDOW, 0)
    number = jnp.sum(flags * jnp.arange(blocks, dtype=jnp.int32))
    amount = jnp.sum(flags)

    def bias_of(query_docs, query_spots, key_docs, key_spots, keep):
        distance = query_spots[:, None] - key_spots[None, :]
        seen = (query_docs[:, None] == key_docs[None, :]) & (distance >= 0) & (distance < WINDOW)
        return jnp.where(seen & keep[:, None], F32(0.0), F32(NEG))

    spots = jnp.arange(rows + WINDOW, dtype=jnp.int32)
    kept = jnp.repeat(flags == 0, block_rows)

    def tile_bias(tile):
        low = tile * TILE
        return bias_of(
            docs[WINDOW + low : WINDOW + low + TILE],
            spots[WINDOW + low : WINDOW + low + TILE],
            docs[low : low + SPAN],
            spots[low : low + SPAN],
            kept[low : low + TILE],
        )

    bias_late = tile_bias(late_tile)
    bias_early = tile_bias(0)
    start = jnp.minimum(number * block_rows, rows + WINDOW - SPAN)
    swap_rows = jnp.tile(lax.dynamic_slice_in_dim(docs, WINDOW + number * block_rows, block_rows, 0), PAIRS)
    swap_spots = jnp.tile(WINDOW + number * block_rows + jnp.arange(block_rows, dtype=jnp.int32), PAIRS)
    bias_swap = bias_of(
        swap_rows,
        swap_spots,
        lax.dynamic_slice_in_dim(docs, start, SPAN, 0),
        start + jnp.arange(SPAN, dtype=jnp.int32),
        jnp.broadcast_to(amount > 0, (PAIRS * block_rows,)),
    )

    tile_cost = pl.CostEstimate(flops=int(6e9), bytes_accessed=2 << 20, transcendentals=1 << 20)
    whole_bias = spec((TILE, SPAN), lambda s, *_: (0, 0))
    scalars = dict(num_scalar_prefetch=2, grid=(HALVES,))

    out_late, dq_late, dkv_late = pl.pallas_call(
        functools.partial(late_kernel, blocks, block_rows),
        grid_spec=pltpu.PrefetchScalarGridSpec(
            **scalars,
            in_specs=[
                half_specs(TILE, wide, late_tile),
                half_specs(TILE, wide, late_tile),
                half_specs(rows, PAIR),
                half_specs(rows, PAIR),
                half_specs(block_rows, 2 * PAIR),
                whole_bias,
            ],
            out_specs=[
                half_specs(TILE, wide, late_tile),
                half_specs(TILE, wide, late_tile),
                half_specs(rows, 2 * PAIR),
            ],
            scratch_shapes=[pltpu.VMEM((rows, 2 * PAIR), BF16)],
        ),
        out_shape=[
            jax.ShapeDtypeStruct((rows, query_width), BF16),
            jax.ShapeDtypeStruct((rows, query_width), BF16),
            jax.ShapeDtypeStruct((rows, 2 * key_width), F32),
        ],
        cost_estimate=tile_cost,
        name="late",
        **params,
    )(flags, sinks, q, g, k, v, kv_in, bias_late)

    qg_in, dkv_late = lax.optimization_barrier((qg_in, dkv_late))

    oq_out, dkv_swap = pl.pallas_call(
        functools.partial(swap_kernel, blocks, block_rows),
        grid_spec=pltpu.PrefetchScalarGridSpec(
            **scalars,
            in_specs=[
                half_specs(block_rows, 2 * wide),
                half_specs(rows, PAIR),
                half_specs(rows, PAIR),
                half_specs(block_rows, 2 * PAIR),
                half_specs(WINDOW + block_rows, 2 * PAIR),
                half_specs(block_rows, 2 * PAIR),
                spec((PAIRS * block_rows, SPAN), lambda s, *_: (0, 0)),
            ],
            out_specs=[half_specs(block_rows, 2 * wide), half_specs(SPAN, 2 * PAIR)],
            scratch_shapes=[pltpu.VMEM((rows + WINDOW, 2 * PAIR), BF16)],
        ),
        out_shape=[
            jax.ShapeDtypeStruct((block_rows, 2 * query_width), BF16),
            jax.ShapeDtypeStruct((SPAN, 2 * key_width), F32),
        ],
        cost_estimate=pl.CostEstimate(flops=int(5e8), bytes_accessed=1 << 20, transcendentals=1 << 18),
        name="swap",
        **params,
    )(flags, sinks, qg_in, k, v, kv_in, tail_in, cross_in, bias_swap)

    oq_in = lax.ppermute(oq_out, "dp", partner)

    out_all, dq_all, dkv_own, back_out, cross_out, trade_out = pl.pallas_call(
        functools.partial(early_kernel, blocks, block_rows),
        grid_spec=pltpu.PrefetchScalarGridSpec(
            **scalars,
            in_specs=[
                half_specs(TILE, wide),
                half_specs(TILE, wide),
                half_specs(rows, PAIR),
                half_specs(rows, PAIR),
                half_specs(block_rows, 2 * PAIR),
                half_specs(WINDOW + block_rows, 2 * PAIR),
                half_specs(block_rows, 2 * PAIR),
                whole_bias,
                half_specs(rows, 2 * PAIR),
                half_specs(SPAN, 2 * PAIR),
                any_spec,
                any_spec,
            ],
            out_specs=[
                half_specs(TILE, wide),
                half_specs(TILE, wide),
                half_specs(rows, 2 * PAIR),
                half_specs(WINDOW, 2 * PAIR),
                half_specs(block_rows, 2 * PAIR),
                half_specs(block_rows, 2 * PAIR),
            ],
            scratch_shapes=[
                pltpu.VMEM((rows + WINDOW, 2 * PAIR), BF16),
                pltpu.VMEM((rows + WINDOW, 2 * PAIR), F32),
            ],
        ),
        out_shape=[
            jax.ShapeDtypeStruct((rows, query_width), BF16),
            jax.ShapeDtypeStruct((rows, query_width), BF16),
            jax.ShapeDtypeStruct((rows, 2 * key_width), F32),
            jax.ShapeDtypeStruct((WINDOW, 2 * key_width), BF16),
            jax.ShapeDtypeStruct((block_rows, 2 * key_width), BF16),
            jax.ShapeDtypeStruct((block_rows, 2 * key_width), BF16),
        ],
        input_output_aliases={12: 0, 13: 1},
        cost_estimate=tile_cost,
        name="early",
        **params,
    )(flags, sinks, q, g, k, v, kv_in, tail_in, cross_in, bias_early, dkv_late, dkv_swap, out_late, dq_late)

    back_in = lax.ppermute(back_out, "ctx", [(target, source) for source, target in forward])
    cross_back = lax.ppermute(cross_out, ("dp", "ctx"), [(target, source) for source, target in across])
    trade_in = lax.ppermute(trade_out, "dp", partner)

    vmem = pl.BlockSpec(memory_space=pltpu.VMEM)
    final = pl.pallas_call(
        functools.partial(finish_kernel, blocks, block_rows),
        in_specs=[pl.BlockSpec(memory_space=pltpu.SMEM)] + [vmem] * 5 + [any_spec] * 2,
        out_specs=[any_spec, any_spec, vmem, vmem],
        out_shape=[
            jax.ShapeDtypeStruct((rows, query_width), BF16),
            jax.ShapeDtypeStruct((rows, query_width), BF16),
            jax.ShapeDtypeStruct((rows, key_width), BF16),
            jax.ShapeDtypeStruct((rows, key_width), BF16),
        ],
        scratch_shapes=[pltpu.SemaphoreType.DMA((2 * HALVES,))],
        input_output_aliases={6: 0, 7: 1},
        cost_estimate=pl.CostEstimate(flops=0, bytes_accessed=1 << 20, transcendentals=0),
        name="finish",
    )(flags, oq_in, dkv_own, back_in, cross_back, trade_in, out_all, dq_all)
    return tuple(array[None] for array in final)


def solution(mesh):
    blocks = P(("groups", "dp"), "ctx", None)
    in_specs = (blocks, blocks, blocks, blocks, P(), P(("groups", "dp"), None), blocks)
    out_specs = (blocks, blocks, blocks, blocks)
    return jax.shard_map(shards, mesh=mesh, in_specs=in_specs, out_specs=out_specs, check_vma=False)
```

time: 98.1 us -> 71.7 us (0.73)
  the two profiles are of different devices: /device:TPU:11 before, /device:TPU:2 now
where the time goes in v1:
time: 71.7 us; the launch traced here: 71.2 us
  Pallas kernels  37.5 us (52%)
  starting transfers between devices  17.4 us (24%)
  local copies, waits for them, and re-layouts  5.9 us (8%)
  waiting for transfers between devices  4.57 us (6%)
  other arithmetic  3.62 us (5%)
  between operations  2.11 us (3%)
    pallas_call x1, Pallas kernels, shards(): pl.pallas_call(functools.partial(early_kernel, blocks, block_rows), grid_...  13.6 us
    pallas_call x1, Pallas kernels, shards(): pl.pallas_call(functools.partial(late_kernel, blocks, block_rows), grid_s...  12.7 us
    pallas_call x1, Pallas kernels, shards(): pl.pallas_call(functools.partial(swap_kernel, blocks, block_rows), grid_s...  6.31 us
    unnamed x22, local copies, waits for them, and re-layouts  4.46 us
    ppermute x1, starting transfers between devices, shards(): lax.ppermute(cross_out, ('dp', 'ctx'), [(target, source) for source, targ...  4.25 us
    ppermute x1, starting transfers between devices, shards(): lax.ppermute(back_out, 'ctx', [(target, source) for source, target in for...  3.31 us
    ppermute x1, waiting for transfers between devices, shards(): trade_in = lax.ppermute(trade_out, 'dp', partner)  3.06 us
    ppermute x1, starting transfers between devices, shards(): kv_in = lax.ppermute(kv_out, 'dp', partner)  2.63 us
  transfers between devices with their start and end apart: 8, of which 2 were waited for; matrix products, arithmetic and copies ran while one was open for 6% of the time, Pallas kernels for 37%

profile of v1, /device:TPU:2, one launch (start us, length us, event | category | flops | bytes accessed | tf_op | source)
XLA Modules:
  0.0 71.2 jit_solution(285175571325457729)
XLA Ops:
  0.6 2.4 %pick.1 = (bf16[16,4096]{1,0:T(8,128)(2,1)}, bf16[16,512]{1,0:T(8,128)(2,1)}, bf16[144,512]{1,0:T(8,128)(2,1)}) custom-call(s32[16]{0:T(128)} %bitcast.33, bf16[256,2048]{1,0:T(8,128)(2,1)} %bitcast.14, bf16[256,2048]{1,0:T(8,128)(2,1)} %bitcast.17, bf16[256,256]{1,0:T(8,128)(2,1)} %bitcast.20, bf16[256,256]{1,0:T(8,128)(2,1)} %bitcast.25, ...), custom_call_target="tpu_custom_call" | custom-call | bytes 1048576 | tf_op jit(solution)/shard_map/pick/pallas_call | solution.py:326
  3.0 2.6 %collective-permute-start.1 = (bf16[16,512]{1,0:T(8,128)(2,1)}, bf16[16,512]{1,0:T(8,128)(2,1)S(1)}, u32[]{:S(2)}, u32[]{:S(2)}) collective-permute-start(bf16[16,512]{1,0:T(8,128)(2,1)} %get-tuple-element.25), channel_id=1, source_target_pairs={{0,8},{4,12},{8,0},{12,4},{1,9},{5,13},{9,1},{13,5},{2,10},{6,14},... | collective-permute-start | bytes 49160 | tf_op jit(solution)/shard_map/ppermute | solution.py:355
  5.6 1.9 %collective-permute-start.3 = (bf16[16,512]{1,0:T(8,128)(2,1)}, bf16[16,512]{1,0:T(8,128)(2,1)S(1)}, u32[]{:S(2)}, u32[]{:S(2)}) collective-permute-start(bf16[16,512]{1,0:T(8,128)(2,1)} %get-tuple-element.25), channel_id=1, source_target_pairs={{0,9},{1,10},{2,11},{4,13},{5,14},{6,15},{8,1},{9,2},{10,3},{12,5}... | collective-permute-start | bytes 49160 | tf_op jit(solution)/shard_map/ppermute | solution.py:357
  7.5 2.1 %collective-permute-start = (bf16[16,4096]{1,0:T(8,128)(2,1)}, bf16[16,4096]{1,0:T(8,128)(2,1)S(1)}, u32[]{:S(2)}, u32[]{:S(2)}) collective-permute-start(bf16[16,4096]{1,0:T(8,128)(2,1)} %get-tuple-element.24), channel_id=1, source_target_pairs={{0,8},{4,12},{8,0},{12,4},{1,9},{5,13},{9,1},{13,5},{2,10},{6,14},... | collective-permute-start | bytes 393224 | tf_op jit(solution)/shard_map/ppermute | solution.py:358
  9.7 1.9 %collective-permute-start.2 = (bf16[144,512]{1,0:T(8,128)(2,1)}, bf16[144,512]{1,0:T(8,128)(2,1)S(1)}, u32[]{:S(2)}, u32[]{:S(2)}) collective-permute-start(bf16[144,512]{1,0:T(8,128)(2,1)} %get-tuple-element.28), channel_id=1, source_target_pairs={{0,1},{1,2},{2,3},{4,5},{5,6},{6,7},{8,9},{9,10},{10,11},{12,13},{... | collective-permute-start | bytes 442376 | tf_op jit(solution)/shard_map/ppermute | solution.py:356
  11.6 0.0 copy-start.2
  11.6 0.7 copy-done.2
  12.3 0.1 pad_dynamic-slice_fusion.2
  12.4 0.6 copy-done.6
  13.1 0.6 multiply_reduce_fusion
  14.4 0.6 reduce_sum.19
  15.0 0.6 copy-done.5
  15.6 0.1 fusion.14
  15.7 0.1 broadcast_in_dim.48
  15.7 0.1 and.44
  15.8 0.1 pad_dynamic-slice_fusion
  15.9 0.1 sub.56
  16.0 0.1 pad_dynamic-slice_fusion.1
  16.1 0.1 eq.48
  16.8 0.1 broadcast_in_dim.53
  16.9 0.1 and.52
  17.0 0.8 %fusion.3.bias_ref = f32[128,256]{1,0:T(8,128)} fusion(s32[256]{0:T(256)S(1)} %slice.45, s32[128]{0:T(128)S(1)} %slice.44, s32[256]{0:T(256)S(1)} %get-tuple-element.47, s32[128]{0:T(128)S(1)} %get-tuple-element.45, pred[128]{0:T(512)(128)(4,1)S(1)} %and.44), kind=kLoop, calls=%fused_computation.7 | loop fusion | flops 262144 | bytes 134272 | tf_op jit(solution)/shard_map/jit(_where)/select_n | solution.py:370
  17.8 0.7 slice-done
  18.4 0.8 %fusion.7.bias_ref = f32[128,256]{1,0:T(8,128)} fusion(s32[256]{0:T(256)S(1)} %slice-done, s32[128]{0:T(128)S(1)} %slice.49, s32[256]{0:T(256)S(1)} %get-tuple-element.46, s32[128]{0:T(128)S(1)} %get-tuple-element.44, pred[128]{0:T(512)(128)(4,1)S(1)} %and.52), kind=kLoop, calls=%fused_computation.11 | loop fusion | flops 262144 | bytes 134272 | tf_op jit(solution)/shard_map/jit(_where)/select_n | solution.py:370
  19.2 0.7 fusion.11.bias_ref
  19.9 0.0 collective-permute-done.1.kv_ref
  19.9 0.6 copy-done.9
  20.5 12.7 %late.1 = (bf16[256,2048]{1,0:T(8,128)(2,1)}, bf16[256,2048]{1,0:T(8,128)(2,1)}, f32[256,512]{1,0:T(8,128)}) custom-call(s32[16]{0:T(128)} %bitcast.34, f32[32]{0:T(128)} %sinks_ref.5, bf16[256,2048]{1,0:T(8,128)(2,1)} %bitcast.15, bf16[256,2048]{1,0:T(8,128)(2,1)} %bitcast.18, bf16[256,256]{1,0:T(8,128)(2,1)} %bitcast.22, bf16[256,256]{1,0:T(8,128)(2,1)} %bitcast.27, ...), custom_call_target="tpu_custom_call" | custom-call | flops 6000000000 | bytes 2097152 | tf_op jit(solution)/shard_map/late/pallas_call | solution.py:402
  33.2 0.0 collective-permute-done.qg_ref
  33.2 0.0 copy-start.8
  33.2 0.0 collective-permute-done.3.cross_ref
  33.3 0.0 collective-permute-done.2.tail_ref
  33.3 0.6 copy-done.8
  33.9 0.7 copy-done.7
  34.6 6.3 %swap.1 = (bf16[16,4096]{1,0:T(8,128)(2,1)}, f32[256,512]{1,0:T(8,128)}) custom-call(s32[16]{0:T(128)} %bitcast.35, f32[32]{0:T(128)} %sinks_ref.5, bf16[16,4096]{1,0:T(8,128)(2,1)} %copy-done.8, bf16[256,256]{1,0:T(8,128)(2,1)} %bitcast.23, bf16[256,256]{1,0:T(8,128)(2,1)} %bitcast.28, bf16[16,512]{1,0:T(8,128)(2,1)} %copy-done.9, ...), custom_call_target="tpu_custom_call" | custom-call | flops 500000000 | bytes 1048576 | tf_op jit(solution)/shard_map/swap/pallas_call | solution.py:433
  40.9 0.9 %collective-permute-start.4 = (bf16[16,4096]{1,0:T(8,128)(2,1)}, bf16[16,4096]{1,0:T(8,128)(2,1)S(1)}, u32[]{:S(2)}, u32[]{:S(2)}) collective-permute-start(bf16[16,4096]{1,0:T(8,128)(2,1)} %get-tuple-element.29), channel_id=1, source_target_pairs={{0,8},{4,12},{8,0},{12,4},{1,9},{5,13},{9,1},{13,5},{2,10},{6,14},... | collective-permute-start | bytes 393224 | tf_op jit(solution)/shard_map/ppermute | solution.py:458
  41.7 13.6 %early.1 = (bf16[256,2048]{1,0:T(8,128)(2,1)}, bf16[256,2048]{1,0:T(8,128)(2,1)}, f32[256,512]{1,0:T(8,128)}, bf16[128,512]{1,0:T(8,128)(2,1)}, bf16[16,512]{1,0:T(8,128)(2,1)}, /*index=5*/bf16[16,512]{1,0:T(8,128)(2,1)}) custom-call(s32[16]{0:T(128)} %bitcast.36, f32[32]{0:T(128)} %sinks_ref.5, ...), custom_call_target="tpu_custom_call", output_to_operand_aliasing={{0}: (12, {}), {1}: (13, {})} | custom-call | flops 6000000000 | bytes 2097152 | tf_op jit(solution)/shard_map/early/pallas_call | solution.py:460
  55.4 3.3 %collective-permute-start.5 = (bf16[128,512]{1,0:T(8,128)(2,1)}, bf16[128,512]{1,0:T(8,128)(2,1)S(1)}, u32[]{:S(2)}, u32[]{:S(2)}) collective-permute-start(bf16[128,512]{1,0:T(8,128)(2,1)} %get-tuple-element.35), channel_id=1, source_target_pairs={{1,0},{2,1},{3,2},{5,4},{6,5},{7,6},{9,8},{10,9},{11,10},{13,12},{... | collective-permute-start | bytes 393224 | tf_op jit(solution)/shard_map/ppermute | solution.py:505
  58.7 4.3 %collective-permute-start.6 = (bf16[16,512]{1,0:T(8,128)(2,1)}, bf16[16,512]{1,0:T(8,128)(2,1)S(1)}, u32[]{:S(2)}, u32[]{:S(2)}) collective-permute-start(bf16[16,512]{1,0:T(8,128)(2,1)} %get-tuple-element.36), channel_id=1, source_target_pairs={{9,0},{10,1},{11,2},{13,4},{14,5},{15,6},{1,8},{2,9},{3,10},{5,12}... | collective-permute-start | bytes 49160 | tf_op jit(solution)/shard_map/ppermute | solution.py:506
  62.9 0.4 collective-permute-start.7
  63.4 1.5 %collective-permute-done.6.cross_ref = bf16[16,512]{1,0:T(8,128)(2,1)S(1)} collective-permute-done((bf16[16,512]{1,0:T(8,128)(2,1)}, bf16[16,512]{1,0:T(8,128)(2,1)S(1)}, u32[]{:S(2)}, u32[]{:S(2)}) %collective-permute-start.6) | collective-permute-done | bytes 16416 | tf_op jit(solution)/shard_map/ppermute | solution.py:506
  64.8 3.1 %collective-permute-done.7.trade_ref = bf16[16,512]{1,0:T(8,128)(2,1)S(1)} collective-permute-done((bf16[16,512]{1,0:T(8,128)(2,1)}, bf16[16,512]{1,0:T(8,128)(2,1)S(1)}, u32[]{:S(2)}, u32[]{:S(2)}) %collective-permute-start.7) | collective-permute-done | bytes 16416 | tf_op jit(solution)/shard_map/ppermute | solution.py:507
  67.9 0.0 collective-permute-done.4.oq_ref
  67.9 0.0 collective-permute-done.5.back_ref
  67.9 0.6 copy-done.4
  68.5 0.1 copy-done
  68.6 0.0 copy-done.1
  68.6 2.5 %finish.1 = (bf16[256,2048]{1,0:T(8,128)(2,1)}, bf16[256,2048]{1,0:T(8,128)(2,1)}, bf16[256,256]{1,0:T(8,128)(2,1)}, bf16[256,256]{1,0:T(8,128)(2,1)}) custom-call(s32[16]{0:T(128)} %bitcast.37, bf16[16,4096]{1,0:T(8,128)(2,1)} %copy-done, f32[256,512]{1,0:T(8,128)} %get-tuple-element.34.own_ref, ...), custom_call_target="tpu_custom_call", output_to_operand_aliasing={{0}: (6, {}), {1}: (7, {})} | custom-call | bytes 1048576 | tf_op jit(solution)/shard_map/finish/pallas_call | solution.py:510
  (23 shorter events, 0.1 us)
Async XLA Ops:
  3.0 16.9 %collective-permute-start.1 = (bf16[16,512]{1,0:T(8,128)(2,1)}, bf16[16,512]{1,0:T(8,128)(2,1)S(1)}, u32[]{:S(2)}, u32[]{:S(2)}) collective-permute-start(bf16[16,512]{1,0:T(8,128)(2,1)} %get-tuple-element.25), channel_id=1, source_target_pairs={{0,8},{4,12},{8,0},{12,4},{1,9},{5,13},{9,1},{13,5},{2,10},{6,14},... | collective-permute-start | bytes 49160 | tf_op jit(solution)/shard_map/ppermute | solution.py:355
  5.6 27.6 %collective-permute-start.3 = (bf16[16,512]{1,0:T(8,128)(2,1)}, bf16[16,512]{1,0:T(8,128)(2,1)S(1)}, u32[]{:S(2)}, u32[]{:S(2)}) collective-permute-start(bf16[16,512]{1,0:T(8,128)(2,1)} %get-tuple-element.25), channel_id=1, source_target_pairs={{0,9},{1,10},{2,11},{4,13},{5,14},{6,15},{8,1},{9,2},{10,3},{12,5}... | collective-permute-start | bytes 49160 | tf_op jit(solution)/shard_map/ppermute | solution.py:357
  7.5 25.7 %collective-permute-start = (bf16[16,4096]{1,0:T(8,128)(2,1)}, bf16[16,4096]{1,0:T(8,128)(2,1)S(1)}, u32[]{:S(2)}, u32[]{:S(2)}) collective-permute-start(bf16[16,4096]{1,0:T(8,128)(2,1)} %get-tuple-element.24), channel_id=1, source_target_pairs={{0,8},{4,12},{8,0},{12,4},{1,9},{5,13},{9,1},{13,5},{2,10},{6,14},... | collective-permute-start | bytes 393224 | tf_op jit(solution)/shard_map/ppermute | solution.py:358
  9.7 23.6 %collective-permute-start.2 = (bf16[144,512]{1,0:T(8,128)(2,1)}, bf16[144,512]{1,0:T(8,128)(2,1)S(1)}, u32[]{:S(2)}, u32[]{:S(2)}) collective-permute-start(bf16[144,512]{1,0:T(8,128)(2,1)} %get-tuple-element.28), channel_id=1, source_target_pairs={{0,1},{1,2},{2,3},{4,5},{5,6},{6,7},{8,9},{9,10},{10,11},{12,13},{... | collective-permute-start | bytes 442376 | tf_op jit(solution)/shard_map/ppermute | solution.py:356
  11.6 0.7 copy-start.2
  12.4 0.7 copy-start.6
  15.0 0.6 copy-start.5
  17.8 0.7 slice-start
  19.9 0.6 copy-start.9
  33.2 0.7 copy-start.8
  33.3 0.6 copy-start.10
  33.9 0.7 copy-start.7
  40.9 27.1 %collective-permute-start.4 = (bf16[16,4096]{1,0:T(8,128)(2,1)}, bf16[16,4096]{1,0:T(8,128)(2,1)S(1)}, u32[]{:S(2)}, u32[]{:S(2)}) collective-permute-start(bf16[16,4096]{1,0:T(8,128)(2,1)} %get-tuple-element.29), channel_id=1, source_target_pairs={{0,8},{4,12},{8,0},{12,4},{1,9},{5,13},{9,1},{13,5},{2,10},{6,14},... | collective-permute-start | bytes 393224 | tf_op jit(solution)/shard_map/ppermute | solution.py:458
  55.4 12.6 %collective-permute-start.5 = (bf16[128,512]{1,0:T(8,128)(2,1)}, bf16[128,512]{1,0:T(8,128)(2,1)S(1)}, u32[]{:S(2)}, u32[]{:S(2)}) collective-permute-start(bf16[128,512]{1,0:T(8,128)(2,1)} %get-tuple-element.35), channel_id=1, source_target_pairs={{1,0},{2,1},{3,2},{5,4},{6,5},{7,6},{9,8},{10,9},{11,10},{13,12},{... | collective-permute-start | bytes 393224 | tf_op jit(solution)/shard_map/ppermute | solution.py:505
  58.7 6.2 %collective-permute-start.6 = (bf16[16,512]{1,0:T(8,128)(2,1)}, bf16[16,512]{1,0:T(8,128)(2,1)S(1)}, u32[]{:S(2)}, u32[]{:S(2)}) collective-permute-start(bf16[16,512]{1,0:T(8,128)(2,1)} %get-tuple-element.36), channel_id=1, source_target_pairs={{9,0},{10,1},{11,2},{13,4},{14,5},{15,6},{1,8},{2,9},{3,10},{5,12}... | collective-permute-start | bytes 49160 | tf_op jit(solution)/shard_map/ppermute | solution.py:506
  62.9 5.0 %collective-permute-start.7 = (bf16[16,512]{1,0:T(8,128)(2,1)}, bf16[16,512]{1,0:T(8,128)(2,1)S(1)}, u32[]{:S(2)}, u32[]{:S(2)}) collective-permute-start(bf16[16,512]{1,0:T(8,128)(2,1)} %get-tuple-element.37), channel_id=1, source_target_pairs={{0,8},{4,12},{8,0},{12,4},{1,9},{5,13},{9,1},{13,5},{2,10},{6,14},... | collective-permute-start | bytes 49160 | tf_op jit(solution)/shard_map/ppermute | solution.py:507
  64.8 3.1 %copy-start.3 = (bf16[16,512]{1,0:T(8,128)(2,1)}, bf16[16,512]{1,0:T(8,128)(2,1)S(1)}, u32[]{:S(2)}) copy-start(bf16[16,512]{1,0:T(8,128)(2,1)S(1)} %collective-permute-done.6.cross_ref) | copy-start | bytes 49156
  67.9 0.6 copy-start.4
  67.9 0.7 copy-start
  67.9 0.7 copy-start.1

commit v2 on v0

v2 whole, which is shorter than its diff:
```python
import functools
import math

import jax
import jax.numpy as jnp
from jax import lax
from jax.experimental import pallas as pl
from jax.experimental.pallas import tpu as pltpu
from jax.sharding import PartitionSpec as P

QUERY_HEADS = 32
KEY_VALUE_HEADS = 4
HEAD_SIZE = 64
WINDOW = 128
TILE = 128
SPAN = TILE + WINDOW
PAIR = 2 * HEAD_SIZE
GROUP = QUERY_HEADS // KEY_VALUE_HEADS
PAIRS = GROUP // 2
NEG = -1e30
SCALE = 1.0 / math.sqrt(HEAD_SIZE)
F32 = jnp.float32
BF16 = jnp.bfloat16


def mm(a, b):
    return lax.dot_general(a, b, (((1,), (0,)), ((), ())), preferred_element_type=F32)


def mm_nt(a, b):
    return lax.dot_general(a, b, (((1,), (1,)), ((), ())), preferred_element_type=F32)


def low_lanes(rows):
    return lax.broadcasted_iota(jnp.int32, (rows, PAIR), 1) < HEAD_SIZE


def spread_head(pair, odd):
    wide = pair.astype(F32)
    low = low_lanes(wide.shape[0])
    if odd:
        high = jnp.where(low, 0.0, wide)
        return pltpu.roll(high, HEAD_SIZE, 1), high
    lower = jnp.where(low, wide, 0.0)
    return lower, pltpu.roll(lower, HEAD_SIZE, 1)


def head_operands(kv, head):
    width = kv.shape[1] // 2
    lanes = slice(head // 2 * PAIR, (head // 2 + 1) * PAIR)
    keys = spread_head(kv[:, lanes], head % 2)
    values = spread_head(kv[:, width + lanes.start : width + lanes.stop], head % 2)
    low = low_lanes(kv.shape[0])
    ones = (jnp.where(low, 1.0, 0.0), jnp.where(low, 0.0, 1.0))
    return (
        jnp.concatenate([part * SCALE for part in keys], axis=0).astype(BF16),
        jnp.concatenate([jnp.concatenate(both, axis=1) for both in zip(values, ones)], axis=0).astype(BF16),
    )


def score_stage(q, operands, bias, sinks):
    found = []
    span = bias.shape[1]
    products = mm_nt(q, operands[0])
    for side, sink in enumerate(sinks):
        scores = products[:, side * span : (side + 1) * span] + bias
        found.append((scores, jnp.maximum(jnp.max(scores, axis=1, keepdims=True), sink)))
    return found


def output_stage(g, operands, found, sinks):
    low = low_lanes(g.shape[0])
    repeats = found[0][0].shape[1] // PAIR
    expos = [jnp.exp(scores - jnp.concatenate([top] * repeats, axis=1)) for scores, top in found]
    rounded = jnp.concatenate([expo.astype(BF16) for expo in expos], axis=1)
    rest = jnp.where(low, jnp.exp(sinks[0] - found[0][1]), jnp.exp(sinks[1] - found[1][1]))
    mixed = mm(rounded, operands[1])
    inverse = 1.0 / (mixed[:, PAIR:] + rest)
    out = (mixed[:, :PAIR] * inverse).astype(BF16)
    weighted = (g.astype(F32) * inverse).astype(BF16)
    product = weighted.astype(F32) * out.astype(F32)
    dots = (
        jnp.sum(jnp.where(low, product, 0.0), axis=1, keepdims=True),
        jnp.sum(jnp.where(low, 0.0, product), axis=1, keepdims=True),
    )
    return out, weighted, expos, rounded, dots


def gradient_stage(q, operands, weighted, expos, rounded, dots):
    span = expos[0].shape[1]
    products = mm_nt(weighted, operands[1][:, :PAIR])
    deltas = jnp.concatenate(
        [
            (expo * (products[:, side * span : (side + 1) * span] - dot)).astype(BF16)
            for side, (expo, dot) in enumerate(zip(expos, dots))
        ],
        axis=1,
    )
    return mm(deltas, operands[0]).astype(BF16), key_sums(q, deltas), key_sums(weighted, rounded)


def key_sums(stacked, both):
    span = both.shape[1] // 2
    turned = jnp.transpose(stacked)
    if stacked.shape[0] % PAIR == 0:
        return mm(
            jnp.concatenate([turned[:HEAD_SIZE], turned[HEAD_SIZE:]], axis=1),
            jnp.concatenate([both[:, :span], both[:, span:]], axis=0),
        )
    return mm(turned[:HEAD_SIZE], both[:, :span]) + mm(turned[HEAD_SIZE:], both[:, span:])


def attend_heads(q_of, g_of, sinks_ref, kv, bias, finish, skew):
    rows = bias.shape[0]
    bias = jnp.concatenate([bias] * PAIRS, axis=0)
    first, second = {}, {}
    dk, dv = [], []
    for step in range(KEY_VALUE_HEADS + 2 * skew):
        head = step
        if head < KEY_VALUE_HEADS:
            spots = [slice((head * PAIRS + pair) * PAIR, (head * PAIRS + pair + 1) * PAIR) for pair in range(PAIRS)]
            q = jnp.concatenate([q_of(spot) for spot in spots], axis=0)
            sinks = [
                jnp.concatenate(
                    [jnp.full((rows, PAIR), sinks_ref[head * GROUP + 2 * pair + side], F32) for pair in range(PAIRS)],
                    axis=0,
                )
                for side in range(2)
            ]
            operands = head_operands(kv, head)
            first[head] = (spots, q, operands, sinks, score_stage(q, operands, bias, sinks))
        head = step - skew
        if 0 <= head < KEY_VALUE_HEADS:
            spots, q, operands, sinks, found = first.pop(head)
            g = jnp.concatenate([g_of(spot) for spot in spots], axis=0)
            second[head] = (spots, q, operands) + output_stage(g, operands, found, sinks)
        head = step - 2 * skew
        if 0 <= head < KEY_VALUE_HEADS:
            spots, q, operands, out, *rest = second.pop(head)
            dq, dk_one, dv_one = gradient_stage(q, operands, *rest)
            finish(head, spots, out, dq)
            dk.append(dk_one)
            dv.append(dv_one)
    turn = lambda parts: jnp.concatenate(
        [jnp.transpose(jnp.concatenate(parts[i : i + 2], axis=0)) for i in range(0, KEY_VALUE_HEADS, 2)], axis=1
    )
    return turn(dk) * SCALE, turn(dv)


def flagged(flags_ref):
    amount = flags_ref[0, 0, 0]
    number = jnp.int32(0)
    for block in range(1, flags_ref.shape[2]):
        amount = amount + flags_ref[0, 0, block]
        number = number + flags_ref[0, 0, block] * block
    return amount, number


def pick_kernel(block_rows, flags_ref, q_ref, g_ref, k_ref, v_ref, qg_ref, kv_ref, tail_ref, sem):
    rows, width = q_ref.shape
    key_width = k_ref.shape[1]
    amount, number = flagged(flags_ref)
    block = pl.ds(pl.multiple_of(number * block_rows, block_rows), block_rows)
    last = slice(rows - WINDOW, rows)
    copies = [
        pltpu.make_async_copy(k_ref.at[last, :], tail_ref.at[:WINDOW, :key_width], sem.at[0]),
        pltpu.make_async_copy(v_ref.at[last, :], tail_ref.at[:WINDOW, key_width:], sem.at[1]),
        pltpu.make_async_copy(k_ref.at[block, :], kv_ref.at[:, :key_width], sem.at[2]),
        pltpu.make_async_copy(v_ref.at[block, :], kv_ref.at[:, key_width:], sem.at[3]),
        pltpu.make_async_copy(q_ref.at[block, :], qg_ref.at[:, :width], sem.at[4]),
        pltpu.make_async_copy(g_ref.at[block, :], qg_ref.at[:, width:], sem.at[5]),
    ]
    for copy in copies:
        copy.start()
    first_tail = (rows - WINDOW) // block_rows
    mark = jnp.where(amount * number >= first_tail, number - first_tail + 1, 0)
    tail_ref[WINDOW:, :] = jnp.full((block_rows, 2 * key_width), mark.astype(F32)).astype(BF16)
    for copy in copies:
        copy.wait()


def fill_keys(block_rows, flags_ref, k_ref, v_ref, kv_ref, kv_scr, base):
    amount, number = flagged(flags_ref)
    rows, key_width = k_ref.shape
    kv_scr[base : base + rows, :key_width] = k_ref[...]
    kv_scr[base : base + rows, key_width:] = v_ref[...]

    @pl.when(amount > 0)
    def _():
        start = pl.multiple_of(base + number * block_rows, block_rows)
        kv_scr[pl.ds(start, block_rows), :] = kv_ref[...]

    return amount, number


def fill_halo(block_rows, tail_ref, cross_ref, kv_scr):
    kv_scr[:WINDOW, :] = tail_ref[:WINDOW, :]
    mark = jnp.max(tail_ref[WINDOW:, :].astype(F32)).astype(jnp.int32)

    @pl.when(mark > 0)
    def _():
        start = pl.multiple_of((mark - 1) * block_rows, block_rows)
        kv_scr[pl.ds(start, block_rows), :] = cross_ref[...]

    return mark


def doc_row(docs_ref, chunk):
    row = docs_ref[pl.ds(jnp.maximum(chunk, 0), 1), :].astype(F32)
    return jnp.where(chunk < 0, -1.0, row)


def doc_column(docs_ref, chunk):
    return jnp.transpose(jnp.broadcast_to(doc_row(docs_ref, chunk), (WINDOW, WINDOW)))


def tile_bias(block_rows, tile, rows, amount, number, docs_ref):
    chunk = lax.axis_index("ctx") * (rows // WINDOW) + tile
    column = doc_column(docs_ref, chunk)
    row = lax.broadcasted_iota(jnp.int32, (TILE, WINDOW), 0)
    lane = lax.broadcasted_iota(jnp.int32, (TILE, WINDOW), 1)
    block = row // block_rows + tile * (TILE // block_rows)
    kept = jnp.logical_or(block != number, amount == 0)
    behind = (column == doc_row(docs_ref, chunk - 1)) & (lane > row) & kept
    beside = (column == doc_row(docs_ref, chunk)) & (lane <= row) & kept
    return jnp.concatenate([jnp.where(behind, 0.0, NEG), jnp.where(beside, 0.0, NEG)], axis=1)


def tile_work(block_rows, tile, flags, sinks_ref, docs_ref, q_ref, g_ref, kv, out_ref, dq_ref, out_scr, dq_scr, sem):
    amount, number = flags
    here = slice(tile * TILE, (tile + 1) * TILE)
    bias = tile_bias(block_rows, tile, q_ref.shape[0], amount, number, docs_ref)
    copies = []

    def finish(head, spots, out, dq):
        for pair, spot in enumerate(spots):
            part = slice(pair * TILE, (pair + 1) * TILE)
            out_scr[:, spot] = out[part]
            dq_scr[:, spot] = dq[part]
        lanes = slice(spots[0].start, spots[-1].stop)
        for side, (source, target) in enumerate(((out_scr, out_ref), (dq_scr, dq_ref))):
            copy = pltpu.make_async_copy(source.at[:, lanes], target.at[here, lanes], sem.at[2 * head + side])
            copy.start()
            copies.append(copy)

    dk, dv = attend_heads(
        lambda spot: q_ref[here, spot], lambda spot: g_ref[here, spot], sinks_ref, kv, bias, finish, 1
    )
    return dk, dv, copies


def late_kernel(
    block_rows, flags_ref, sinks_ref, docs_ref, q_ref, g_ref, k_ref, v_ref, kv_ref,
    out_ref, dq_ref, dkv_ref, kv_scr, out_scr, dq_scr, sem,
):
    rows, key_width = k_ref.shape
    flags = fill_keys(block_rows, flags_ref, k_ref, v_ref, kv_ref, kv_scr, 0)
    dk, dv, copies = tile_work(
        block_rows, rows // TILE - 1, flags, sinks_ref, docs_ref, q_ref, g_ref, kv_scr[rows - SPAN :, :],
        out_ref, dq_ref, out_scr, dq_scr, sem,
    )
    dkv_ref[:, :key_width] = dk
    dkv_ref[:, key_width:] = dv
    for copy in copies:
        copy.wait()


def swap_kernel(
    block_rows, flags_ref, sinks_ref, docs_ref, qg_ref, k_ref, v_ref, kv_ref, tail_ref, cross_ref,
    oq_ref, dkv_ref, kv_scr, doc_scr,
):
    rows, key_width = k_ref.shape
    width = qg_ref.shape[1] // 2
    amount, number = fill_keys(block_rows, flags_ref, k_ref, v_ref, kv_ref, kv_scr, WINDOW)
    fill_halo(block_rows, tail_ref, cross_ref, kv_scr)
    chunk = lax.axis_index("ctx") * (rows // WINDOW)
    per = WINDOW // block_rows
    doc_scr[...] = doc_column(docs_ref, chunk + number // per)
    column = doc_scr[pl.ds(pl.multiple_of(number % per * block_rows, block_rows), block_rows), :]
    row = lax.broadcasted_iota(jnp.int32, (block_rows, WINDOW), 0) + (WINDOW + number * block_rows)
    lane = lax.broadcasted_iota(jnp.int32, (block_rows, WINDOW), 1)
    parts = []
    for part in range(rows // WINDOW + 1):
        distance = row - lane - part * WINDOW
        seen = (column == doc_row(docs_ref, chunk + part - 1)) & (distance >= 0) & (distance < WINDOW) & (amount > 0)
        parts.append(jnp.where(seen, 0.0, NEG))

    def finish(head, spots, out, dq):
        for pair, spot in enumerate(spots):
            part = slice(pair * block_rows, (pair + 1) * block_rows)
            oq_ref[:, spot] = out[part]
            oq_ref[:, width + spot.start : width + spot.stop] = dq[part]

    dk, dv = attend_heads(
        lambda spot: qg_ref[:, spot],
        lambda spot: qg_ref[:, width + spot.start : width + spot.stop],
        sinks_ref, kv_scr[...], jnp.concatenate(parts, axis=1), finish, 1,
    )
    dkv_ref[:, :key_width] = dk
    dkv_ref[:, key_width:] = dv


def early_kernel(
    block_rows, flags_ref, sinks_ref, docs_ref, q_ref, g_ref, k_ref, v_ref, kv_ref, tail_ref, cross_ref,
    late_ref, swap_ref, out_in, dq_in, out_ref, dq_ref, own_ref, back_ref, cross_back_ref, trade_ref,
    kv_scr, dkv_scr, out_scr, dq_scr, sem,
):
    rows, key_width = k_ref.shape
    flags = fill_keys(block_rows, flags_ref, k_ref, v_ref, kv_ref, kv_scr, WINDOW)
    mark = fill_halo(block_rows, tail_ref, cross_ref, kv_scr)
    dk, dv, copies = tile_work(
        block_rows, 0, flags, sinks_ref, docs_ref, q_ref, g_ref, kv_scr[:SPAN, :], out_ref, dq_ref, out_scr, dq_scr, sem
    )
    dkv = jnp.concatenate([dk, dv], axis=1) + swap_ref[:SPAN, :]
    late = late_ref.shape[0] - (rows + WINDOW - SPAN)
    dkv_scr[:WINDOW, :] = dkv[:WINDOW]
    dkv_scr[WINDOW:SPAN, :] = dkv[WINDOW:] + late_ref[:late, :]
    dkv_scr[SPAN:, :] = late_ref[late:, :] + swap_ref[SPAN:, :]
    own_ref[...] = dkv_scr[WINDOW:, :]
    back_ref[...] = dkv[:WINDOW].astype(BF16)
    spot = pl.multiple_of(WINDOW + flags[1] * block_rows, block_rows)
    trade_ref[...] = dkv_scr[pl.ds(spot, block_rows), :].astype(BF16)
    cross = pl.multiple_of(jnp.maximum(mark - 1, 0) * block_rows, block_rows)
    cross_back_ref[...] = dkv_scr[pl.ds(cross, block_rows), :].astype(BF16)
    for copy in copies:
        copy.wait()


def finish_kernel(
    block_rows, flags_ref, oq_ref, own_ref, back_ref, cross_ref, trade_ref, out_in, dq_in,
    out_ref, dq_ref, dk_ref, dv_ref, sem,
):
    amount, number = flagged(flags_ref)
    start = pl.multiple_of(number * block_rows, block_rows)
    width = oq_ref.shape[1] // 2
    copies = [
        pltpu.make_async_copy(
            oq_ref.at[:, side * width : (side + 1) * width], target.at[pl.ds(start, block_rows), :], sem.at[side]
        )
        for side, target in enumerate((out_ref, dq_ref))
    ]

    @pl.when(amount > 0)
    def _():
        for copy in copies:
            copy.start()

    rows, key_width = dk_ref.shape
    tail = rows - WINDOW
    for side, target in enumerate((dk_ref, dv_ref)):
        lanes = slice(side * key_width, (side + 1) * key_width)
        target[:tail, :] = own_ref[:tail, lanes].astype(BF16)
        target[tail:, :] = (own_ref[tail:, lanes] + back_ref[:, lanes].astype(F32)).astype(BF16)

    @pl.when(amount > 0)
    def _():
        tail_part = jnp.where(start >= tail, 1.0, 0.0)
        total = (trade_ref[...].astype(F32) + tail_part * cross_ref[...].astype(F32)).astype(BF16)
        dk_ref[pl.ds(start, block_rows), :] = total[:, :key_width]
        dv_ref[pl.ds(start, block_rows), :] = total[:, key_width:]
        for copy in copies:
            copy.wait()


def shards(queries, keys, values, grad_out, sinks, doc_ids, swap_flags):
    rows, width = queries.shape[1:]
    key_width = keys.shape[2]
    block_rows = rows // swap_flags.shape[2]
    q, k, v, g = queries[0], keys[0], values[0], grad_out[0]
    docs = doc_ids.reshape(doc_ids.shape[1] // WINDOW, WINDOW)
    packs = lax.axis_size("dp")
    runs = lax.axis_size("ctx")
    partner = [(rank, (rank + packs // 2) % packs) for rank in range(packs)]
    forward = [(run, (run + 1) % runs) for run in range(runs)]
    across = [
        (rank * runs + run, (rank + packs // 2) % packs * runs + (run + 1) % runs)
        for rank in range(packs)
        for run in range(runs)
    ]
    reverse = lambda pairs: [(target, source) for source, target in pairs]

    vmem = pl.BlockSpec(memory_space=pltpu.VMEM)
    smem = pl.BlockSpec(memory_space=pltpu.SMEM)
    anywhere = pl.BlockSpec(memory_space=pltpu.HBM)
    wide = jax.ShapeDtypeStruct((rows, width), BF16)

    def call(body, name, in_specs, out_specs, out_shape, scratch, cost, mib, aliases={}):
        return pl.pallas_call(
            functools.partial(body, block_rows),
            in_specs=in_specs,
            out_specs=out_specs,
            out_shape=out_shape,
            scratch_shapes=scratch,
            input_output_aliases=aliases,
            cost_estimate=pl.CostEstimate(flops=int(cost), bytes_accessed=1 << 20, transcendentals=0),
            compiler_params=pltpu.CompilerParams(vmem_limit_bytes=mib << 20),
            name=name,
        )

    def made(height, lanes, dtype=BF16):
        return jax.ShapeDtypeStruct((height, lanes), dtype)

    qg_out, kv_out, tail_out = call(
        pick_kernel, "pick", [smem] + [anywhere] * 4, [vmem] * 3,
        [made(block_rows, 2 * width), made(block_rows, 2 * key_width), made(WINDOW + block_rows, 2 * key_width)],
        [pltpu.SemaphoreType.DMA((6,))], 1e6, 4,
    )(swap_flags, q, g, k, v)

    kv_in = lax.ppermute(kv_out, "dp", partner)
    cross_in = lax.ppermute(kv_out, ("dp", "ctx"), across)
    tail_in = lax.ppermute(tail_out, "ctx", forward)
    qg_in = lax.ppermute(qg_out, "dp", partner)

    tile_scratch = [
        pltpu.VMEM((TILE, width), BF16),
        pltpu.VMEM((TILE, width), BF16),
        pltpu.SemaphoreType.DMA((2 * KEY_VALUE_HEADS,)),
    ]
    head = [smem, smem, vmem]
    out_late, dq_late, dkv_late = call(
        late_kernel, "late", head + [vmem] * 5, [anywhere, anywhere, vmem],
        [wide, wide, made(SPAN, 2 * key_width, F32)],
        [pltpu.VMEM((rows, 2 * key_width), BF16)] + tile_scratch, 6e9, 24,
    )(swap_flags, sinks, docs, q, g, k, v, kv_in)

    qg_in, dkv_late = lax.optimization_barrier((qg_in, dkv_late))

    oq_out, dkv_swap = call(
        swap_kernel, "swap", head + [vmem] * 6, [vmem, vmem],
        [made(block_rows, 2 * width), made(rows + WINDOW, 2 * key_width, F32)],
        [pltpu.VMEM((rows + WINDOW, 2 * key_width), BF16), pltpu.VMEM((WINDOW, WINDOW), F32)], 1e9, 16,
    )(swap_flags, sinks, docs, qg_in, k, v, kv_in, tail_in, cross_in)

    oq_in = lax.ppermute(oq_out, "dp", partner)

    out_all, dq_all, dkv_own, back_out, cross_out, trade_out = call(
        early_kernel, "early", head + [vmem] * 9 + [anywhere] * 2, [anywhere, anywhere] + [vmem] * 4,
        [
            wide,
            wide,
            made(rows, 2 * key_width, F32),
            made(WINDOW, 2 * key_width),
            made(block_rows, 2 * key_width),
            made(block_rows, 2 * key_width),
        ],
        [pltpu.VMEM((rows + WINDOW, 2 * key_width), BF16), pltpu.VMEM((rows + WINDOW, 2 * key_width), F32)] + tile_scratch,
        6e9, 24, {12: 0, 13: 1},
    )(swap_flags, sinks, docs, q, g, k, v, kv_in, tail_in, cross_in, dkv_late, dkv_swap, out_late, dq_late)

    back_in = lax.ppermute(back_out, "ctx", reverse(forward))
    cross_back = lax.ppermute(cross_out, ("dp", "ctx"), reverse(across))
    trade_in = lax.ppermute(trade_out, "dp", partner)

    final = call(
        finish_kernel, "finish", [smem] + [vmem] * 5 + [anywhere] * 2, [anywhere, anywhere, vmem, vmem],
        [wide, wide, made(rows, key_width), made(rows, key_width)],
        [pltpu.SemaphoreType.DMA((2,))], 1e6, 4, {6: 0, 7: 1},
    )(swap_flags, oq_in, dkv_own, back_in, cross_back, trade_in, out_all, dq_all)
    return tuple(array[None] for array in final)


def solution(mesh):
    blocks = P(("groups", "dp"), "ctx", None)
    in_specs = (blocks, blocks, blocks, blocks, P(), P(("groups", "dp"), None), blocks)
    out_specs = (blocks, blocks, blocks, blocks)
    return jax.shard_map(shards, mesh=mesh, in_specs=in_specs, out_specs=out_specs, check_vma=False)
```

time: 98.1 us -> 39.6 us (0.40)
  the two profiles are of different devices: /device:TPU:11 before, /device:TPU:0 now
where the time goes in v2:
time: 39.6 us; the launch traced here: 39.4 us
  Pallas kernels  16.2 us (41%)
  starting transfers between devices  11.8 us (30%)
  waiting for transfers between devices  5.75 us (15%)
  local copies, waits for them, and re-layouts  4.93 us (12%)
  between operations  0.73 us (2%)
    pallas_call x1, Pallas kernels, shards(): call(early_kernel, 'early', head + [vmem] * 9 + [anywhere] * 2, [anywhere...  5.43 us
    pallas_call x1, Pallas kernels, shards(): call(late_kernel, 'late', head + [vmem] * 5, [anywhere, anywhere, vmem],...  5.29 us
    unnamed x22, local copies, waits for them, and re-layouts  4.93 us
    ppermute x1, starting transfers between devices, shards(): kv_in = lax.ppermute(kv_out, 'dp', partner)  4.13 us
    ppermute x1, waiting for transfers between devices, shards(): trade_in = lax.ppermute(trade_out, 'dp', partner)  3.2 us
    ppermute x1, starting transfers between devices, shards(): cross_back = lax.ppermute(cross_out, ('dp', 'ctx'), reverse(across))  3.16 us
    pallas_call x1, Pallas kernels, shards(): call(swap_kernel, 'swap', head + [vmem] * 6, [vmem, vmem], [made(block_ro...  2.78 us
    ppermute x1, starting transfers between devices, shards(): qg_in = lax.ppermute(qg_out, 'dp', partner)  2.08 us
  transfers between devices with their start and end apart: 8, of which 3 were waited for; matrix products, arithmetic and copies ran while one was open for 0% of the time, Pallas kernels for 27%

profile of v2, /device:TPU:0, one launch (start us, length us, event | category | flops | bytes accessed | tf_op | source)
XLA Modules:
  0.0 39.4 jit_solution(16215918057292786268)
XLA Ops:
  0.6 0.0 copy-start.8
  0.6 0.6 %copy-done.8 = s32[1,1,16]{2,1,0:T(1,128)S(1)} copy-done((s32[1,1,16]{2,1,0:T(1,128)S(1)}, s32[1,1,16]{2,1,0:T(1,128)}, u32[]{:S(2)}) %copy-start.8) | copy-done | bytes 88
  1.3 0.0 copy-start
  1.3 1.2 %copy-done = bf16[1,256,2048]{2,1,0:T(8,128)(2,1)S(1)} copy-done((bf16[1,256,2048]{2,1,0:T(8,128)(2,1)S(1)}, bf16[1,256,2048]{2,1,0:T(8,128)(2,1)}, u32[]{:S(2)}) %copy-start) | copy-done | bytes 1048600
  2.5 0.0 copy-start.2
  2.5 1.2 %copy-done.2 = bf16[1,256,2048]{2,1,0:T(8,128)(2,1)S(1)} copy-done((bf16[1,256,2048]{2,1,0:T(8,128)(2,1)S(1)}, bf16[1,256,2048]{2,1,0:T(8,128)(2,1)}, u32[]{:S(2)}) %copy-start.2) | copy-done | bytes 1048600
  3.7 0.0 copy-start.4
  3.7 0.9 %copy-done.4 = bf16[1,256,256]{2,1,0:T(8,128)(2,1)S(1)} copy-done((bf16[1,256,256]{2,1,0:T(8,128)(2,1)S(1)}, bf16[1,256,256]{2,1,0:T(8,128)(2,1)}, u32[]{:S(2)}) %copy-start.4) | copy-done | bytes 131096
  4.6 0.0 copy-start.6
  4.6 0.9 %copy-done.6 = bf16[1,256,256]{2,1,0:T(8,128)(2,1)S(1)} copy-done((bf16[1,256,256]{2,1,0:T(8,128)(2,1)S(1)}, bf16[1,256,256]{2,1,0:T(8,128)(2,1)}, u32[]{:S(2)}) %copy-start.6) | copy-done | bytes 131096
  5.5 0.0 copy-start.1
  5.6 0.0 copy-start.3
  5.6 0.0 copy-start.5
  5.6 0.0 copy-start.7
  5.6 0.8 %pick.1 = (bf16[16,4096]{1,0:T(8,128)(2,1)S(1)}, bf16[16,512]{1,0:T(8,128)(2,1)S(1)}, bf16[144,512]{1,0:T(8,128)(2,1)S(1)}) custom-call(s32[1,1,16]{2,1,0:T(1,128)S(1)} %copy-done.8, bf16[256,2048]{1,0:T(8,128)(2,1)S(1)} %bitcast.9, bf16[256,2048]{1,0:T(8,128)(2,1)S(1)} %bitcast.12, bf16[256,256]{1,0:T(8,128)(2,1)S(1)} %bitcast.15, bf16[256,256]{1,0:T(8,128)(2,1)S(1)} %bitcast.19), custom_call_target="tpu_custom_call" | custom-call | flops 1000000 | bytes 1048576 | tf_op jit(solution)/shard_map/pick/pallas_call | solution.py:403
  6.3 0.0 copy-start.9
  6.3 4.1 %collective-permute-start.1 = (bf16[16,512]{1,0:T(8,128)(2,1)S(1)}, bf16[16,512]{1,0:T(8,128)(2,1)S(1)}, u32[]{:S(2)}, u32[]{:S(2)}) collective-permute-start(bf16[16,512]{1,0:T(8,128)(2,1)S(1)} %get-tuple-element.25), channel_id=1, source_target_pairs={{0,8},{4,12},{8,0},{12,4},{1,9},{5,13},{9,1},{13,5},{2,10},{6,14},... | collective-permute-start | bytes 49160 | tf_op jit(solution)/shard_map/ppermute | solution.py:409
  10.5 0.0 collective-permute-start.3
  10.5 2.1 %collective-permute-start = (bf16[16,4096]{1,0:T(8,128)(2,1)S(1)}, bf16[16,4096]{1,0:T(8,128)(2,1)S(1)}, u32[]{:S(2)}, u32[]{:S(2)}) collective-permute-start(bf16[16,4096]{1,0:T(8,128)(2,1)S(1)} %get-tuple-element.24), channel_id=1, source_target_pairs={{0,8},{4,12},{8,0},{12,4},{1,9},{5,13},{9,1},{13,5},{2,10},{6,14},... | collective-permute-start | bytes 393224 | tf_op jit(solution)/shard_map/ppermute | solution.py:412
  12.6 0.0 copy-start.10
  12.6 1.6 %collective-permute-start.2 = (bf16[144,512]{1,0:T(8,128)(2,1)S(1)}, bf16[144,512]{1,0:T(8,128)(2,1)S(1)}, u32[]{:S(2)}, u32[]{:S(2)}) collective-permute-start(bf16[144,512]{1,0:T(8,128)(2,1)S(1)} %get-tuple-element.28), channel_id=1, source_target_pairs={{0,1},{1,2},{2,3},{3,0},{4,5},{5,6},{6,7},{7,4},{8,9},{9,10},{10,1... | collective-permute-start | bytes 442376 | tf_op jit(solution)/shard_map/ppermute | solution.py:411
  14.2 0.0 collective-permute-done.1.kv_ref
  14.2 0.0 copy-done.1
  14.2 0.0 copy-done.3
  14.2 0.0 copy-done.5
  14.2 0.0 copy-done.7
  14.2 0.0 copy-done.9
  14.2 0.0 copy-done.10
  14.2 5.3 %late.1 = (bf16[256,2048]{1,0:T(8,128)(2,1)}, bf16[256,2048]{1,0:T(8,128)(2,1)}, f32[256,512]{1,0:T(8,128)S(1)}) custom-call(s32[1,1,16]{2,1,0:T(1,128)S(1)} %copy-done.8, f32[32]{0:T(128)S(1)} %copy-done.10, s32[8,128]{1,0:T(8,128)S(1)} %bitcast.23, bf16[256,2048]{1,0:T(8,128)(2,1)S(1)} %bitcast.10, bf16[256,2048]{1,0:T(8,128)(2,1)S(1)} %bitcast.13, ...), custom_call_target="tpu_custom_call" | custom-call | flops 6000000000 | bytes 1048576 | tf_op jit(solution)/shard_map/late/pallas_call | solution.py:420
  19.5 1.1 %collective-permute-done.qg_ref = bf16[16,4096]{1,0:T(8,128)(2,1)S(1)} collective-permute-done((bf16[16,4096]{1,0:T(8,128)(2,1)S(1)}, bf16[16,4096]{1,0:T(8,128)(2,1)S(1)}, u32[]{:S(2)}, u32[]{:S(2)}) %collective-permute-start) | collective-permute-done | bytes 131104 | tf_op jit(solution)/shard_map/ppermute | solution.py:412
  20.6 0.0 collective-permute-done.3.cross_ref
  20.6 0.0 collective-permute-done.2.tail_ref
  20.6 2.8 %swap.1 = (bf16[16,4096]{1,0:T(8,128)(2,1)S(1)}, f32[384,512]{1,0:T(8,128)S(1)}) custom-call(s32[1,1,16]{2,1,0:T(1,128)S(1)} %copy-done.8, f32[32]{0:T(128)S(1)} %copy-done.10, s32[8,128]{1,0:T(8,128)S(1)} %bitcast.24, bf16[16,4096]{1,0:T(8,128)(2,1)S(1)} %collective-permute-done.qg_ref, bf16[256,256]{1,0:T(8,128)(2,1)S(1)} %bitcast.17, ...), custom_call_target="tpu_custom_call" | custom-call | flops 1000000000 | bytes 1048576 | tf_op jit(solution)/shard_map/swap/pallas_call | solution.py:428
  23.4 0.1 collective-permute-start.4
  23.5 5.4 %early.1 = (bf16[256,2048]{1,0:T(8,128)(2,1)}, bf16[256,2048]{1,0:T(8,128)(2,1)}, f32[256,512]{1,0:T(8,128)S(1)}, bf16[128,512]{1,0:T(8,128)(2,1)S(1)}, bf16[16,...) custom-call(s32[1,1,16]{2,1,0:T(1,128)S(1)} %copy-done.8, ...), custom_call_target="tpu_custom_call", output_to_operand_aliasing={{0}: (12, {}), {1}: (13, {})} | custom-call | flops 6000000000 | bytes 1048576 | tf_op jit(solution)/shard_map/early/pallas_call | solution.py:436
  28.9 0.7 %collective-permute-start.5 = (bf16[128,512]{1,0:T(8,128)(2,1)S(1)}, bf16[128,512]{1,0:T(8,128)(2,1)S(1)}, u32[]{:S(2)}, u32[]{:S(2)}) collective-permute-start(bf16[128,512]{1,0:T(8,128)(2,1)S(1)} %get-tuple-element.35), channel_id=1, source_target_pairs={{1,0},{2,1},{3,2},{0,3},{5,4},{6,5},{7,6},{4,7},{9,8},{10,9},{11,1... | collective-permute-start | bytes 393224 | tf_op jit(solution)/shard_map/ppermute | solution.py:450
  29.6 3.2 %collective-permute-start.6 = (bf16[16,512]{1,0:T(8,128)(2,1)S(1)}, bf16[16,512]{1,0:T(8,128)(2,1)S(1)}, u32[]{:S(2)}, u32[]{:S(2)}) collective-permute-start(bf16[16,512]{1,0:T(8,128)(2,1)S(1)} %get-tuple-element.36), channel_id=1, source_target_pairs={{9,0},{10,1},{11,2},{8,3},{13,4},{14,5},{15,6},{12,7},{1,8},{2,9},... | collective-permute-start | bytes 49160 | tf_op jit(solution)/shard_map/ppermute | solution.py:451
  32.8 0.0 collective-permute-start.7
  32.8 1.4 %collective-permute-done.6.cross_ref = bf16[16,512]{1,0:T(8,128)(2,1)S(1)} collective-permute-done((bf16[16,512]{1,0:T(8,128)(2,1)S(1)}, bf16[16,512]{1,0:T(8,128)(2,1)S(1)}, u32[]{:S(2)}, u32[]{:S(2)}) %collective-permute-start.6) | collective-permute-done | bytes 16416 | tf_op jit(solution)/shard_map/ppermute | solution.py:451
  34.2 3.2 %collective-permute-done.7.trade_ref = bf16[16,512]{1,0:T(8,128)(2,1)S(1)} collective-permute-done((bf16[16,512]{1,0:T(8,128)(2,1)S(1)}, bf16[16,512]{1,0:T(8,128)(2,1)S(1)}, u32[]{:S(2)}, u32[]{:S(2)}) %collective-permute-start.7) | collective-permute-done | bytes 16416 | tf_op jit(solution)/shard_map/ppermute | solution.py:452
  37.4 0.0 collective-permute-done.4.oq_ref
  37.4 0.0 collective-permute-done.5.back_ref
  37.4 1.9 %finish.1 = (bf16[256,2048]{1,0:T(8,128)(2,1)}, bf16[256,2048]{1,0:T(8,128)(2,1)}, bf16[256,256]{1,0:T(8,128)(2,1)}, bf16[256,256]{1,0:T(8,128)(2,1)}) custom-call(s32[1,1,16]{2,1,0:T(1,128)S(1)} %copy-done.8, bf16[16,4096]{1,0:T(8,128)(2,1)S(1)} %collective-permute-done.4.oq_ref, ...), custom_call_target="tpu_custom_call", output_to_operand_aliasing={{0}: (6, {}), {1}: (7, {})} | custom-call | flops 1000000 | bytes 1048576 | tf_op jit(solution)/shard_map/finish/pallas_call | solution.py:454
Async XLA Ops:
  0.6 0.7 %copy-start.8 = (s32[1,1,16]{2,1,0:T(1,128)S(1)}, s32[1,1,16]{2,1,0:T(1,128)}, u32[]{:S(2)}) copy-start(s32[1,1,16]{2,1,0:T(1,128)} %flags_ref.9) | copy-start | bytes 196
  1.3 1.2 %copy-start = (bf16[1,256,2048]{2,1,0:T(8,128)(2,1)S(1)}, bf16[1,256,2048]{2,1,0:T(8,128)(2,1)}, u32[]{:S(2)}) copy-start(bf16[1,256,2048]{2,1,0:T(8,128)(2,1)} %param.7) | copy-start | bytes 3145732
  2.5 1.2 %copy-start.2 = (bf16[1,256,2048]{2,1,0:T(8,128)(2,1)S(1)}, bf16[1,256,2048]{2,1,0:T(8,128)(2,1)}, u32[]{:S(2)}) copy-start(bf16[1,256,2048]{2,1,0:T(8,128)(2,1)} %param.10) | copy-start | bytes 3145732
  3.7 0.9 %copy-start.4 = (bf16[1,256,256]{2,1,0:T(8,128)(2,1)S(1)}, bf16[1,256,256]{2,1,0:T(8,128)(2,1)}, u32[]{:S(2)}) copy-start(bf16[1,256,256]{2,1,0:T(8,128)(2,1)} %param.8) | copy-start | bytes 393220
  4.6 0.9 %copy-start.6 = (bf16[1,256,256]{2,1,0:T(8,128)(2,1)S(1)}, bf16[1,256,256]{2,1,0:T(8,128)(2,1)}, u32[]{:S(2)}) copy-start(bf16[1,256,256]{2,1,0:T(8,128)(2,1)} %param.9) | copy-start | bytes 393220
  5.5 8.6 %copy-start.1 = (bf16[1,256,2048]{2,1,0:T(8,128)(2,1)S(1)}, bf16[1,256,2048]{2,1,0:T(8,128)(2,1)}, u32[]{:S(2)}) copy-start(bf16[1,256,2048]{2,1,0:T(8,128)(2,1)} %param.7) | copy-start | bytes 3145732
  5.6 8.6 %copy-start.3 = (bf16[1,256,2048]{2,1,0:T(8,128)(2,1)S(1)}, bf16[1,256,2048]{2,1,0:T(8,128)(2,1)}, u32[]{:S(2)}) copy-start(bf16[1,256,2048]{2,1,0:T(8,128)(2,1)} %param.10) | copy-start | bytes 3145732
  5.6 8.6 %copy-start.5 = (bf16[1,256,256]{2,1,0:T(8,128)(2,1)S(1)}, bf16[1,256,256]{2,1,0:T(8,128)(2,1)}, u32[]{:S(2)}) copy-start(bf16[1,256,256]{2,1,0:T(8,128)(2,1)} %param.8) | copy-start | bytes 393220
  5.6 8.6 %copy-start.7 = (bf16[1,256,256]{2,1,0:T(8,128)(2,1)S(1)}, bf16[1,256,256]{2,1,0:T(8,128)(2,1)}, u32[]{:S(2)}) copy-start(bf16[1,256,256]{2,1,0:T(8,128)(2,1)} %param.9) | copy-start | bytes 393220
  6.3 7.9 %copy-start.9 = (s32[1,1024]{1,0:T(1,128)S(1)}, s32[1,1024]{1,0:T(1,128)}, u32[]{:S(2)}) copy-start(s32[1,1024]{1,0:T(1,128)} %param.12) | copy-start | bytes 12292
  6.3 7.8 %collective-permute-start.1 = (bf16[16,512]{1,0:T(8,128)(2,1)S(1)}, bf16[16,512]{1,0:T(8,128)(2,1)S(1)}, u32[]{:S(2)}, u32[]{:S(2)}) collective-permute-start(bf16[16,512]{1,0:T(8,128)(2,1)S(1)} %get-tuple-element.25), channel_id=1, source_target_pairs={{0,8},{4,12},{8,0},{12,4},{1,9},{5,13},{9,1},{13,5},{2,10},{6,14},... | collective-permute-start | bytes 49160 | tf_op jit(solution)/shard_map/ppermute | solution.py:409
  10.5 10.2 %collective-permute-start.3 = (bf16[16,512]{1,0:T(8,128)(2,1)S(1)}, bf16[16,512]{1,0:T(8,128)(2,1)S(1)}, u32[]{:S(2)}, u32[]{:S(2)}) collective-permute-start(bf16[16,512]{1,0:T(8,128)(2,1)S(1)} %get-tuple-element.25), channel_id=1, source_target_pairs={{0,9},{1,10},{2,11},{3,8},{4,13},{5,14},{6,15},{7,12},{8,1},{9,2},... | collective-permute-start | bytes 49160 | tf_op jit(solution)/shard_map/ppermute | solution.py:410
  10.5 10.2 %collective-permute-start = (bf16[16,4096]{1,0:T(8,128)(2,1)S(1)}, bf16[16,4096]{1,0:T(8,128)(2,1)S(1)}, u32[]{:S(2)}, u32[]{:S(2)}) collective-permute-start(bf16[16,4096]{1,0:T(8,128)(2,1)S(1)} %get-tuple-element.24), channel_id=1, source_target_pairs={{0,8},{4,12},{8,0},{12,4},{1,9},{5,13},{9,1},{13,5},{2,10},{6,14},... | collective-permute-start | bytes 393224 | tf_op jit(solution)/shard_map/ppermute | solution.py:412
  12.6 1.6 %copy-start.10 = (f32[32]{0:T(128)S(1)}, f32[32]{0:T(128)}, u32[]{:S(2)}) copy-start(f32[32]{0:T(128)} %sinks_ref.5) | copy-start | bytes 388
  12.6 8.1 %collective-permute-start.2 = (bf16[144,512]{1,0:T(8,128)(2,1)S(1)}, bf16[144,512]{1,0:T(8,128)(2,1)S(1)}, u32[]{:S(2)}, u32[]{:S(2)}) collective-permute-start(bf16[144,512]{1,0:T(8,128)(2,1)S(1)} %get-tuple-element.28), channel_id=1, source_target_pairs={{0,1},{1,2},{2,3},{3,0},{4,5},{5,6},{6,7},{7,4},{8,9},{9,10},{10,1... | collective-permute-start | bytes 442376 | tf_op jit(solution)/shard_map/ppermute | solution.py:411
  23.4 14.0 %collective-permute-start.4 = (bf16[16,4096]{1,0:T(8,128)(2,1)S(1)}, bf16[16,4096]{1,0:T(8,128)(2,1)S(1)}, u32[]{:S(2)}, u32[]{:S(2)}) collective-permute-start(bf16[16,4096]{1,0:T(8,128)(2,1)S(1)} %get-tuple-element.29), channel_id=1, source_target_pairs={{0,8},{4,12},{8,0},{12,4},{1,9},{5,13},{9,1},{13,5},{2,10},{6,14},... | collective-permute-start | bytes 393224 | tf_op jit(solution)/shard_map/ppermute | solution.py:434
  28.9 8.5 %collective-permute-start.5 = (bf16[128,512]{1,0:T(8,128)(2,1)S(1)}, bf16[128,512]{1,0:T(8,128)(2,1)S(1)}, u32[]{:S(2)}, u32[]{:S(2)}) collective-permute-start(bf16[128,512]{1,0:T(8,128)(2,1)S(1)} %get-tuple-element.35), channel_id=1, source_target_pairs={{1,0},{2,1},{3,2},{0,3},{5,4},{6,5},{7,6},{4,7},{9,8},{10,9},{11,1... | collective-permute-start | bytes 393224 | tf_op jit(solution)/shard_map/ppermute | solution.py:450
  29.6 4.6 %collective-permute-start.6 = (bf16[16,512]{1,0:T(8,128)(2,1)S(1)}, bf16[16,512]{1,0:T(8,128)(2,1)S(1)}, u32[]{:S(2)}, u32[]{:S(2)}) collective-permute-start(bf16[16,512]{1,0:T(8,128)(2,1)S(1)} %get-tuple-element.36), channel_id=1, source_target_pairs={{9,0},{10,1},{11,2},{8,3},{13,4},{14,5},{15,6},{12,7},{1,8},{2,9},... | collective-permute-start | bytes 49160 | tf_op jit(solution)/shard_map/ppermute | solution.py:451
  32.8 4.6 %collective-permute-start.7 = (bf16[16,512]{1,0:T(8,128)(2,1)S(1)}, bf16[16,512]{1,0:T(8,128)(2,1)S(1)}, u32[]{:S(2)}, u32[]{:S(2)}) collective-permute-start(bf16[16,512]{1,0:T(8,128)(2,1)S(1)} %get-tuple-element.37), channel_id=1, source_target_pairs={{0,8},{4,12},{8,0},{12,4},{1,9},{5,13},{9,1},{13,5},{2,10},{6,14},... | collective-permute-start | bytes 49160 | tf_op jit(solution)/shard_map/ppermute | solution.py:452
